TPU v7x, 1024 devices: a whole 4x4x32 slice. The times are simulated.
1024 devices in a mesh: doc: 32 (over z), fsdp: 32 (over x, y, core).
Axes of the slice: x: 4, y: 4, z: 32, core: 2. Of those that a mesh axis runs over, the one named last changes fastest.
Arguments:
- tokens_in: bfloat16 [32, 256, 4096], P('doc'), may hold values from -6 to 6
- mix_in: bfloat16 [32, 256, 8192], P('doc', None, 'fsdp'), may hold values from -6 to 6
- step_size: float32 [32, 256, 128], P('doc', None, 'fsdp'), may hold values from 0.0025 to 0.03
- doc_ids: int32 [32, 256], P('doc'), may hold values from 0 to 3, never falling along the last dimension, each value on 1 to 128 neighbouring positions
- out_grad: bfloat16 [32, 256, 8192], P('doc', None, 'fsdp'), may hold values from -6 to 6
- proj_weight: bfloat16 [4096, 256], P('fsdp'), may hold values from -0.046875 to 0.046875
- conv_weight: float32 [4, 8192], P(None, 'fsdp'), may hold values from -3 to 3
- decay_rate: float32 [128], P('fsdp'), may hold values from 0.02 to 2.5
- carried_state: bfloat16 [32, 128, 64, 128], P(None, 'fsdp', 'doc'), may hold values from -3 to 3
- carried_conv: bfloat16 [32, 3, 128, 64], P(None, None, 'fsdp', 'doc'), may hold values from -6 to 6
- carry_from: int32 [32], replicated, may hold values from -1 to 31, as said below
Outputs:
- grad_proj: float32 [4096, 256], P(('doc', 'fsdp'))
- grad_state: bfloat16 [32, 128, 64, 128], P(None, 'fsdp', 'doc')
- grad_conv: bfloat16 [32, 3, 128, 64], P(None, None, 'fsdp', 'doc')
Inputs may be any that keep to these rules, and one draw needn't show every extreme that they name: `carry_from`: each row names the slot of the previous window that its first document continues, or -1 if it starts fresh; no slot is named by two rows.
All inputs are finite; a program needn't handle non-finite values.
Results may differ from a plain program's by a relative error of at most 0.007.
Values may be sent and summed in bfloat16 or wider, within the bound.
No kernel may reach another device: no remote copies, remote signals or barrier semaphores. Data moves between devices by JAX's collectives and lax.ppermute only.
A program may use at most 32 MiB of HBM per device.

v0:
```python
import jax
import jax.numpy as jnp
from jax import lax
from jax.sharding import PartitionSpec as P


def silu_slope(value):
    sigmoid_value = jax.nn.sigmoid(value)
    return sigmoid_value * (1.0 + value * (1.0 - sigmoid_value))


def conv_masks(seg_row, tap_count):
    length = seg_row.shape[0]
    opening = seg_row == seg_row[0]
    tap_masks = []
    for offset in range(tap_count):
        earlier = jnp.concatenate([jnp.full((offset,), -1, jnp.int32), seg_row[: length - offset]])
        inside = jnp.arange(length) >= offset
        tap_masks.append(jnp.where(inside, earlier == seg_row, opening))
    return (opening, tap_masks)


def row_pass(
    coeff, mix_row, step_row, seg_row, grad_rows, state_zero, conv_zero, conv_weight, decay_rate
):
    length, channels = mix_row.shape
    head_count = step_row.shape[1]
    head_dim = channels // head_count
    tap_count = conv_weight.shape[0]
    nstate = coeff.shape[1] // 2
    opening, tap_masks = conv_masks(seg_row, tap_count)
    extended = jnp.concatenate([conv_zero, mix_row], axis=0).astype(jnp.float32)
    preact = jnp.zeros((length, channels), jnp.float32)
    for offset in range(tap_count):
        window = extended[tap_count - 1 - offset : tap_count - 1 - offset + length]
        preact = preact + jnp.where(
            tap_masks[offset][:, None], conv_weight[offset][None, :] * window, 0.0
        )
    mixed_rows = jax.nn.silu(preact).astype(jnp.bfloat16)
    values = (
        step_row[:, :, None] * mixed_rows.reshape(length, head_count, head_dim).astype(jnp.float32)
    ).astype(jnp.bfloat16)
    write_coeff = coeff[:, :nstate]
    read_coeff = coeff[:, nstate:]
    scores = jnp.dot(read_coeff, write_coeff.T, preferred_element_type=jnp.float32)
    log_decay = jnp.cumsum(-(decay_rate[None, :] * step_row), axis=0).T
    lower = jnp.arange(length)[:, None] >= jnp.arange(length)[None, :]
    allowed = lower & (seg_row[:, None] == seg_row[None, :])
    spread = log_decay[:, :, None] - log_decay[:, None, :]
    decays = jnp.where(allowed[None], jnp.exp(jnp.where(allowed[None], spread, 0.0)), 0.0)
    edge_weight = jnp.where(opening[None, :], jnp.exp(log_decay), 0.0)
    weighted = (decays * scores[None]).astype(jnp.bfloat16)
    grad_heads = grad_rows.reshape(length, head_count, head_dim)
    values_grad = jnp.einsum(
        "hts,thp->shp", weighted, grad_heads, preferred_element_type=jnp.float32
    )
    products = jnp.einsum("thp,shp->hts", grad_heads, values, preferred_element_type=jnp.float32)
    score_grad = jnp.sum(decays * products, axis=0)
    carried = jnp.einsum("thp,hpn->thn", grad_heads, state_zero, preferred_element_type=jnp.float32)
    read_grad = jnp.dot(
        score_grad, write_coeff.astype(jnp.float32), precision=lax.Precision.HIGHEST
    )
    read_grad = read_grad + jnp.sum(edge_weight.T[:, :, None] * carried, axis=1)
    write_grad = jnp.dot(
        score_grad.T, read_coeff.astype(jnp.float32), precision=lax.Precision.HIGHEST
    )
    scaled = edge_weight.T[:, :, None] * grad_heads.astype(jnp.float32)
    state_grad = jnp.einsum(
        "thp,tn->hpn", scaled, read_coeff.astype(jnp.float32), precision=lax.Precision.HIGHEST
    )
    mixed_grad = (values_grad * step_row[:, :, None]).reshape(length, channels)
    preact_grad = mixed_grad * silu_slope(preact)
    conv_rows = []
    for index_row in range(tap_count - 1):
        running = jnp.zeros((channels,), jnp.float32)
        for offset in range(tap_count - 1 - index_row, tap_count):
            position = index_row - (tap_count - 1) + offset
            running = running + jnp.where(
                opening[position], conv_weight[offset] * preact_grad[position], 0.0
            )
        conv_rows.append(running)
    conv_grad = jnp.stack(conv_rows)
    return (jnp.concatenate([write_grad, read_grad], axis=1), state_grad, conv_grad)


def shards(
    tokens_in,
    mix_in,
    step_size,
    doc_ids,
    out_grad,
    proj_weight,
    conv_weight,
    decay_rate,
    carried_state,
    carried_conv,
    carry_from,
):
    rows_dev, length, model_width = tokens_in.shape
    head_count = step_size.shape[2]
    slot_count = carried_state.shape[0]
    part_p = carried_state.shape[2]
    nstate = carried_state.shape[3]
    tap_count = conv_weight.shape[0]
    doc_count = lax.axis_size("doc")
    fsdp_count = lax.axis_size("fsdp")
    head_dim = part_p * doc_count
    channels = head_count * head_dim
    picker = (carry_from[:, None] == jnp.arange(slot_count, dtype=jnp.int32)[None, :]).astype(
        jnp.bfloat16
    )
    chosen_state = jnp.einsum(
        "rs,shpn->rhpn", picker, carried_state, preferred_element_type=jnp.float32
    ).astype(jnp.bfloat16)
    chosen_conv = jnp.einsum(
        "rs,skhp->rkhp", picker, carried_conv, preferred_element_type=jnp.float32
    ).astype(jnp.bfloat16)
    chosen_state = chosen_state.reshape(slot_count, head_count, part_p * nstate)
    chosen_conv = chosen_conv.reshape(slot_count, (tap_count - 1) * head_count, part_p)
    start_state, start_conv = (
        lax.all_to_all(chosen_state, "doc", split_axis=0, concat_axis=2, tiled=True),
        lax.all_to_all(chosen_conv, "doc", split_axis=0, concat_axis=2, tiled=True),
    )
    start_state = start_state.reshape(rows_dev, head_count, head_dim, nstate)
    start_conv = start_conv.reshape(rows_dev, tap_count - 1, channels)
    flattened = tokens_in.reshape(rows_dev * length, model_width)
    columns = flattened
    coeff_sum = jnp.dot(
        columns,
        lax.all_gather(proj_weight, "fsdp", axis=0, tiled=True),
        preferred_element_type=jnp.float32,
    )
    coeff = coeff_sum.astype(jnp.bfloat16).reshape(rows_dev, length, proj_weight.shape[1])
    coeff_grad, state_grad, conv_grad = row_pass(
        coeff[0],
        mix_in[0],
        step_size[0],
        doc_ids[0],
        out_grad[0],
        start_state[0],
        start_conv[0],
        conv_weight,
        decay_rate,
    )
    coeff_grads = [coeff_grad]
    state_grads = [state_grad]
    conv_grads = [conv_grad]
    back_state = (
        jnp.stack(state_grads).astype(jnp.bfloat16).reshape(rows_dev, head_count, head_dim * nstate)
    )
    back_conv = (
        jnp.stack(conv_grads)
        .astype(jnp.bfloat16)
        .reshape(rows_dev, (tap_count - 1) * head_count, head_dim)
    )
    got_state, got_conv = (
        lax.all_to_all(back_state, "doc", split_axis=2, concat_axis=0, tiled=True),
        lax.all_to_all(back_conv, "doc", split_axis=2, concat_axis=0, tiled=True),
    )
    grad_state = jnp.einsum(
        "rs,rx->sx", picker, got_state.reshape(slot_count, -1), preferred_element_type=jnp.float32
    )
    grad_state = grad_state.astype(jnp.bfloat16).reshape(carried_state.shape)
    grad_conv = jnp.einsum(
        "rs,rx->sx", picker, got_conv.reshape(slot_count, -1), preferred_element_type=jnp.float32
    )
    grad_conv = grad_conv.astype(jnp.bfloat16).reshape(carried_conv.shape)
    coeff_flat = jnp.stack(coeff_grads).reshape(rows_dev * length, -1)
    rows_own = model_width // (doc_count * fsdp_count)
    summed = lax.psum(coeff_flat, "fsdp")
    blocked = flattened.reshape(rows_dev * length, doc_count, fsdp_count, rows_own)
    columns = lax.dynamic_index_in_dim(blocked, lax.axis_index("fsdp"), 2, keepdims=False)
    partial_rows = jnp.einsum(
        "tdj,tn->djn", columns.astype(jnp.float32), summed, precision=lax.Precision.HIGHEST
    )
    grad_proj = lax.psum_scatter(partial_rows, "doc", scatter_dimension=0, tiled=True).reshape(
        rows_own, -1
    )
    return (grad_proj, grad_state, grad_conv)


def solution(mesh):
    return jax.shard_map(
        shards,
        mesh=mesh,
        in_specs=(
            P("doc", None, None),
            P("doc", None, "fsdp"),
            P("doc", None, "fsdp"),
            P("doc", None),
            P("doc", None, "fsdp"),
            P("fsdp", None),
            P(None, "fsdp"),
            P("fsdp"),
            P(None, "fsdp", "doc", None),
            P(None, None, "fsdp", "doc"),
            P(),
        ),
        out_specs=(
            P(("doc", "fsdp"), None),
            P(None, "fsdp", "doc", None),
            P(None, None, "fsdp", "doc"),
        ),
        check_vma=False,
    )
```

profile of v0, /device:TPU:6, one launch (start us, length us, event | category | flops | bytes accessed | tf_op | source)
XLA Modules:
  0.0 598.3 jit_solution(12811974616221853607)
XLA Ops:
  7.2 0.7 all-gather.2.cloned.1.call-update
  7.9 0.9 convolution_convert_fusion.4
  8.8 0.7 copy.111
  9.5 28.7 %all-to-all-start = ((bf16[32,12,2]{1,2,0:T(2,128)(2,1)}), bf16[32,12,2]{1,2,0:T(2,128)(2,1)S(1)}, u32[]{:S(2)}, u32[]{:S(2)}) async-start(bf16[32,12,2]{1,2,0:T(2,128)(2,1)} %copy.111), calls=%async_computation | async-start | bytes 32768 | tf_op jit(solution)/shard_map/all_to_all | solution.py:122
  38.3 1.2 slice.91
  39.4 0.8 negate_bitcast_fusion
  40.2 1.2 reduce-window.6
  41.4 0.1 slice.110
  41.5 0.1 copy.107
  41.7 0.1 copy.108
  41.8 1.3 compare_reduce_fusion
  43.1 0.8 fusion.57
  44.0 0.1 add_bitcast_fusion
  44.0 0.9 convolution_convert_fusion.1
  44.9 1.6 broadcast_compare_fusion
  46.5 0.7 reshape.194
  47.2 13.5 %all-to-all-done = bf16[32,12,2]{1,2,0:T(2,128)(2,1)S(1)} async-done(((bf16[32,12,2]{1,2,0:T(2,128)(2,1)}), bf16[32,12,2]{1,2,0:T(2,128)(2,1)S(1)}, u32[]{:S(2)}, u32[]{:S(2)}) %all-to-all-start) | async-done | bytes 1568 | tf_op jit(solution)/shard_map/all_to_all | solution.py:122
  60.7 8.3 %all-to-all-start.1 = ((bf16[32,4,256]{2,1,0:T(4,128)(2,1)}), bf16[32,4,256]{2,1,0:T(4,128)(2,1)S(1)}, u32[]{:S(2)}, u32[]{:S(2)}) async-start(bf16[32,4,256]{2,1,0:T(4,128)(2,1)} %reshape.194), calls=%async_computation.1 | async-start | bytes 131072 | tf_op jit(solution)/shard_map/all_to_all | solution.py:121
  69.0 0.7 fusion.58
  69.6 1.0 copy.114
  70.7 3.3 copy.105
  74.0 2.1 reshape_reshape.3
  76.0 1.3 dynamic-slice
  77.3 0.9 constant_dynamic-slice_fusion
  78.2 0.1 fusion.25
  78.3 0.3 copy.112
  78.7 0.2 squeeze_reshape.6
  78.9 15.3 %all-to-all-done.1 = bf16[32,4,256]{2,1,0:T(4,128)(2,1)S(1)} async-done(((bf16[32,4,256]{2,1,0:T(4,128)(2,1)}), bf16[32,4,256]{2,1,0:T(4,128)(2,1)S(1)}, u32[]{:S(2)}, u32[]{:S(2)}) %all-to-all-start.1) | async-done | bytes 65568 | tf_op jit(solution)/shard_map/all_to_all | solution.py:121
  94.3 0.3 fusion.5
  94.6 4.2 all-gather.2.cloned.1.call-done
  98.7 2.9 fusion.7
  101.7 0.2 fusion.33
  101.9 0.5 fusion.6
  102.4 0.1 copy.126
  102.5 0.3 multiply_multiply_fusion
  102.8 2.0 fusion.49
  104.8 0.1 convert_element_type.70
  104.9 0.7 copy.127
  105.6 23.0 %all-to-all-start.3 = ((bf16[1,12,64]{1,0,2:T(2,128)(2,1)}), bf16[1,12,64]{1,0,2:T(2,128)(2,1)S(1)}, u32[]{:S(2)}, u32[]{:S(2)}) async-start(bf16[1,12,64]{1,0,2:T(2,128)(2,1)} %copy.127), calls=%async_computation.3 | async-start | bytes 65536 | tf_op jit(solution)/shard_map/all_to_all | solution.py:158
  128.6 0.2 all-reduce.6.cloned.1.call-start
  128.9 0.1 fusion.26
  128.9 0.1 copy.113
  129.1 0.5 fusion.3
  129.5 0.3 fusion.38
  129.8 0.3 convolution_add_fusion
  130.1 0.7 pad_maximum_fusion
  130.9 0.3 convolution_convert_fusion.2
  131.2 6.9 %copy.121 = bf16[1,4,8192]{1,0,2:T(2,128)(2,1)} copy(bf16[1,4,8192]{2,1,0:T(4,128)(2,1)S(1)} %reshape.184) | data formatting | bytes 131072 | tf_op jit(solution)/shard_map/reshape | solution.py:149
  138.1 0.5 broadcast.74
  138.6 45.2 %reduce.2 = bf16[8192,4]{1,0:T(8,128)(2,1)S(1)} reduce(bf16[8192,1,4]{2,1,0:T(2,128)(2,1)} %bitcast.120, bf16[]{:T(256)} %broadcast.74), dimensions={1}, to_apply=%bitcast.103.reduce_sub_computation | reduce | bytes 131074
  183.8 4.6 reshape.197
  188.4 21.8 %all-to-all-start.2 = ((bf16[32,2,512]{2,1,0:T(2,128)(2,1)}), bf16[32,2,512]{2,1,0:T(2,128)(2,1)S(1)}, u32[]{:S(2)}, u32[]{:S(2)}) async-start(bf16[32,2,512]{2,1,0:T(2,128)(2,1)} %reshape.197), calls=%async_computation.2 | async-start | bytes 131072 | tf_op jit(solution)/shard_map/all_to_all | solution.py:157
  210.3 0.1 copy.128
  210.4 96.2 %all-reduce.6.cloned.1.call-done = f32[256,256]{0,1:T(8,128)} async-done(((f32[256,256]{0,1:T(8,128)}), f32[256,256]{0,1:T(8,128)}) %all-reduce.6.cloned.1.call-update) | async-done | bytes 262160 | tf_op jit(solution)/shard_map/psum | solution.py:170
  306.5 1.2 fusion.21
  307.8 0.7 copy.120
  308.6 0.8 convolution_convert_fusion.3
  309.3 262.6 %all-reduce.8.cloned.1.call-done = f32[32,4,256]{2,1,0:T(4,128)} async-done(((f32[32,4,256]{2,1,0:T(4,128)}), f32[32,4,256]{2,1,0:T(4,128)}) %all-reduce.8.cloned.1.call-update) | async-done | bytes 131088
  572.0 1.9 dynamic-slice_bitcast_fusion
  573.9 8.7 %reshape.198 = bf16[8192,1,4]{2,1,0:T(2,128)(2,1)} reshape(bf16[32,2,512]{2,1,0:T(2,128)(2,1)S(1)} %all-to-all-done.2) | data formatting | bytes 131072
  582.6 8.1 %copy.122 = bf16[1,4,8192]{2,1,0:T(4,128)(2,1)S(1)} copy(bf16[1,4,8192]{1,0,2:T(2,128)(2,1)} %bitcast.121) | data formatting | bytes 131072 | tf_op jit(solution)/shard_map/all_to_all | solution.py:157
  590.7 0.1 copy.123
  590.8 0.3 convolution_convert_fusion
  591.1 0.7 reshape.186
  (33 shorter events, 0.4 us)
Async XLA Ops:
  7.2 36.9 %copy-start = (bf16[32,4,2,128]{3,2,1,0:T(2,128)(2,1)S(1)}, bf16[32,4,2,128]{3,2,1,0:T(2,128)(2,1)}, u32[]{:S(2)}) copy-start(bf16[32,4,2,128]{3,2,1,0:T(2,128)(2,1)} %param.19) | copy-start | bytes 196612
  7.2 91.6 %all-gather.2.cloned.1.call-start = ((), (), s32[]{:S(2)}) async-start(), calls=%async_computation.4 | async-start | bytes 2162688 | tf_op jit(solution)/shard_map/all_gather | solution.py:130
  9.5 51.2 %all-to-all-start = ((bf16[32,12,2]{1,2,0:T(2,128)(2,1)}), bf16[32,12,2]{1,2,0:T(2,128)(2,1)S(1)}, u32[]{:S(2)}, u32[]{:S(2)}) async-start(bf16[32,12,2]{1,2,0:T(2,128)(2,1)} %copy.111), calls=%async_computation | async-start | bytes 32768 | tf_op jit(solution)/shard_map/all_to_all | solution.py:122
  60.7 33.5 %all-to-all-start.1 = ((bf16[32,4,256]{2,1,0:T(4,128)(2,1)}), bf16[32,4,256]{2,1,0:T(4,128)(2,1)S(1)}, u32[]{:S(2)}, u32[]{:S(2)}) async-start(bf16[32,4,256]{2,1,0:T(4,128)(2,1)} %reshape.194), calls=%async_computation.1 | async-start | bytes 131072 | tf_op jit(solution)/shard_map/all_to_all | solution.py:121
  73.9 4.3 copy-start.2
  74.0 4.9 copy-start.1
  94.5 7.3 %copy-start.4 = (f32[1,256,4]{1,2,0:T(4,128)S(1)}, f32[1,256,4]{1,2,0:T(4,128)}, u32[]{:S(2)}) copy-start(f32[1,256,4]{1,2,0:T(4,128)} %param.13) | copy-start | bytes 12292
  101.9 0.9 copy-start.3
  105.6 82.8 %all-to-all-start.3 = ((bf16[1,12,64]{1,0,2:T(2,128)(2,1)}), bf16[1,12,64]{1,0,2:T(2,128)(2,1)S(1)}, u32[]{:S(2)}, u32[]{:S(2)}) async-start(bf16[1,12,64]{1,0,2:T(2,128)(2,1)} %copy.127), calls=%async_computation.3 | async-start | bytes 65536 | tf_op jit(solution)/shard_map/all_to_all | solution.py:158
  128.6 177.9 %all-reduce.6.cloned.1.call-start = ((), (), s32[]{:S(2)}) async-start(), calls=%async_computation.5 | async-start | bytes 524288 | tf_op jit(solution)/shard_map/psum | solution.py:170
  183.8 124.8 %copy-start.5 = (s32[32]{0:T(128)S(1)}, s32[32]{0:T(128)}, u32[]{:S(2)}) copy-start(s32[32]{0:T(128)} %param.21) | copy-start | bytes 388
  188.4 385.5 %all-to-all-start.2 = ((bf16[32,2,512]{2,1,0:T(2,128)(2,1)}), bf16[32,2,512]{2,1,0:T(2,128)(2,1)S(1)}, u32[]{:S(2)}, u32[]{:S(2)}) async-start(bf16[32,2,512]{2,1,0:T(2,128)(2,1)} %reshape.197), calls=%async_computation.2 | async-start | bytes 131072 | tf_op jit(solution)/shard_map/all_to_all | solution.py:157
  210.2 361.8 %all-reduce.8.cloned.1.call-start = ((), (), s32[]{:S(2)}) async-start(), calls=%async_computation.6 | async-start | bytes 262144
Sparse Core Ops, SparseCore 0:
  12.3 86.4 all-gather.1
  132.7 173.8 all-reduce.5
  308.9 263.0 all-reduce.7
where the time goes:
time: 599 us; the launch traced here: 598 us
  waiting for transfers between devices  393 us (66%)
  starting transfers between devices  82.1 us (14%)
  other arithmetic  53.4 us (9%)
  local copies, waits for them, and re-layouts  46.8 us (8%)
  between operations  14.1 us (2%)
  matrix products  9.23 us (2%)
    unnamed x4, waiting for transfers between devices  263 us
    psum x1, waiting for transfers between devices, shards(): summed = lax.psum(coeff_flat, 'fsdp')  96.2 us
    unnamed x2, other arithmetic  45.3 us
    all_to_all x1, starting transfers between devices, shards(): lax.all_to_all(chosen_conv, 'doc', split_axis=0, concat_axis=2, tiled=True)  28.7 us
    all_to_all x1, starting transfers between devices, shards(): lax.all_to_all(back_conv, 'doc', split_axis=2, concat_axis=0, tiled=True)  23 us
    all_to_all x1, starting transfers between devices, shards(): lax.all_to_all(back_state, 'doc', split_axis=2, concat_axis=0, tiled=True)  21.8 us
    unnamed x22, local copies, waits for them, and re-layouts  19.5 us
    all_to_all x1, waiting for transfers between devices, shards(): lax.all_to_all(chosen_state, 'doc', split_axis=0, concat_axis=2, tiled=True)  15.3 us
  transfers between devices with their start and end apart: 7, of which 5 were waited for; matrix products, arithmetic and copies ran while one was open for 14% of the time, Pallas kernels for 0%

commit v1 on v0

v1 whole, which is shorter than its diff:
```python
import jax
import jax.numpy as jnp
from jax import lax
from jax.experimental import pallas as pl
from jax.experimental.pallas import tpu as pltpu
from jax.sharding import PartitionSpec as P

INTERPRET = False
F32 = jnp.float32
BF16 = jnp.bfloat16


def iota(shape, dim):
    return lax.broadcasted_iota(jnp.int32, shape, dim)


def one_hot(condition):
    return jnp.where(condition, 1.0, 0.0).astype(BF16)


def dot(a, b):
    return jnp.dot(a, b, preferred_element_type=F32)


def dot_nt(a, b, precision=None):
    return lax.dot_general(
        a, b, (((1,), (1,)), ((), ())), precision=precision, preferred_element_type=F32
    )


def halves(value):
    high = value.astype(BF16)
    return high, (value - high.astype(F32)).astype(BF16)


def call(body, out_shape, in_specs, scratch=()):
    vmem = pl.BlockSpec(memory_space=pltpu.VMEM)
    smem = pl.BlockSpec(memory_space=pltpu.SMEM)
    many = isinstance(out_shape, tuple)
    return pl.pallas_call(
        body,
        out_shape=out_shape,
        in_specs=[smem if spec == "s" else vmem for spec in in_specs],
        out_specs=tuple(vmem for _ in out_shape) if many else vmem,
        scratch_shapes=list(scratch),
        interpret=INTERPRET,
    )


def shaped(shape, kind):
    return jax.ShapeDtypeStruct(shape, kind)


def pick_body(carry_ref, slots_ref, picked_ref):
    for r in range(picked_ref.shape[0]):
        source = carry_ref[r]
        row = slots_ref[jnp.maximum(source, 0)]
        picked_ref[r] = jnp.where(source >= 0, row, jnp.zeros_like(row))


def turn_body(weight_ref, turned_ref):
    rows, columns = weight_ref.shape
    turned = weight_ref[...].astype(F32).T
    turned_ref[...] = turned.reshape(columns // 8, 8, rows).astype(BF16)


def coeff_body(weight_ref, tokens_ref, copies_ref):
    parts = weight_ref.shape[0]
    weight = jnp.concatenate([weight_ref[i] for i in range(parts)], axis=1)
    column = dot_nt(weight, tokens_ref[...]).astype(BF16)
    for i in range(parts):
        copies_ref[i] = column


def row_body(
    decay_ref,
    coeff_ref,
    mix_ref,
    step_ref,
    doc_ref,
    grad_ref,
    tap_ref,
    start_ref,
    coeff_grad_ref,
    state_ref,
    conv_ref,
    ext,
    doc_ext,
):
    length, channels = mix_ref.shape
    heads = step_ref.shape[1]
    head_dim = channels // heads
    taps = tap_ref.shape[0]
    docs = start_ref.shape[0]
    part_p = head_dim // docs
    rows_in = heads * part_p
    nstate = start_ref.shape[2]
    square = (length, channels)

    start = start_ref[...].astype(F32)
    state_in = start[:, :rows_in].reshape(channels, nstate).astype(BF16)
    conv_in = jnp.sum(start[:, rows_in:], axis=1).astype(BF16)
    chan = iota((channels, channels), 0)
    other = iota((channels, channels), 1)
    place = (
        ((chan % head_dim) // part_p) * rows_in + (chan // head_dim) * part_p + chan % part_p
    )
    to_natural = one_hot(place == other)
    place_t = (
        ((other % head_dim) // part_p) * rows_in + (other // head_dim) * part_p + other % part_p
    )
    to_parts = one_hot(place_t == chan)
    state_zero = dot(to_natural, state_in).astype(BF16)
    lane_chan = iota((nstate, channels), 1)
    lane = iota((nstate, channels), 0)
    lane_of = (lane_chan // head_dim) * part_p + lane_chan % part_p
    owner = (iota((docs, channels), 1) % head_dim) // part_p == iota((docs, channels), 0)
    sub = iota((8, channels), 0)
    head_rows = jnp.zeros((8, channels), F32)
    for k in range(taps - 1):
        spread_row = dot(conv_in, one_hot(lane == k * rows_in + lane_of))
        line = jnp.sum(jnp.where(owner, spread_row, 0.0), axis=0, keepdims=True)
        head_rows = jnp.where(sub == 8 - (taps - 1) + k, line, head_rows)

    doc_row = doc_ref[...]
    doc_turned = jnp.broadcast_to(doc_row.astype(F32), (128, length)).T
    doc_col = jnp.concatenate([doc_turned] * (channels // 128), axis=1)
    doc_first = doc_row[0:1, 0:1].astype(F32)
    opening = doc_col == doc_first
    doc_ext[0:8] = jnp.broadcast_to(doc_first, (8, channels))
    doc_ext[8:] = doc_col

    ext[0:8] = head_rows
    ext[8:] = mix_ref[...].astype(F32)
    preact = jnp.zeros(square, F32)
    for k in range(taps):
        same = doc_ext[8 - k : 8 - k + length] == doc_col
        term = tap_ref[k : k + 1] * ext[8 - k : 8 - k + length]
        preact = preact + jnp.where(same, term, 0.0)
    head_of = iota(square, 1) // head_dim
    step = jnp.broadcast_to(step_ref[:, 0:1], square)
    rate = jnp.where(head_of[0:1] == 0, decay_ref[0], 0.0)
    for h in range(1, heads):
        step = jnp.where(head_of == h, step_ref[:, h : h + 1], step)
        rate = jnp.where(head_of[0:1] == h, decay_ref[h], rate)
    gate = 1.0 / (1.0 + jnp.exp(-preact))
    mixed = (preact * gate).astype(BF16).astype(F32)
    values = (step * mixed).astype(BF16)

    time_row = iota((length, length), 0)
    time_col = iota((length, length), 1)
    lower = time_row >= time_col
    lower_one = one_hot(lower)
    change = -(rate * step)
    first = change.astype(BF16)
    rest = change - first.astype(F32)
    second, third = halves(rest)
    log_decay = dot(lower_one, first) + (dot(lower_one, second) + dot(lower_one, third))
    log_turned = log_decay.T
    allowed = lower & (doc_col == doc_row.astype(F32))
    grad = grad_ref[...]
    grad_wide = grad.astype(F32)
    score_grad = jnp.zeros((length, length), F32)
    for h in range(heads):
        own = jnp.where(head_of == h, grad_wide, 0.0).astype(BF16)
        products = dot_nt(own, values)
        column = log_decay[:, h * head_dim : h * head_dim + 1]
        spread = column - log_turned[h * head_dim : h * head_dim + 1]
        decays = jnp.where(allowed, jnp.exp(jnp.where(allowed, spread, 0.0)), 0.0)
        score_grad = score_grad + decays * products

    coeff = coeff_ref[...].astype(F32).reshape(2 * nstate, length)
    write_turned = coeff[:nstate]
    read_turned = coeff[nstate:]
    write = write_turned.T.astype(BF16)
    read = read_turned.T.astype(BF16)
    read_turned = read_turned.astype(BF16)

    edge = jnp.where(opening, jnp.exp(log_decay), 0.0)
    scaled_high, scaled_low = halves(edge * grad_wide)
    score_high, score_low = halves(score_grad)
    read_grad = dot(score_high, write) + dot(score_low, write)
    read_grad = read_grad + dot(scaled_high, state_zero) + dot(scaled_low, state_zero)
    write_grad = dot(read_turned, score_high) + dot(read_turned, score_low)
    coeff_grad = jnp.concatenate([write_grad, read_grad.T], axis=0)
    coeff_grad_ref[...] = coeff_grad.reshape(coeff_grad_ref.shape).astype(BF16)
    state_grad = dot(read_turned, scaled_high) + dot(read_turned, scaled_low)
    state_grad = state_grad.T.astype(BF16)
    state_ref[...] = dot(to_parts, state_grad).reshape(state_ref.shape).astype(BF16)

    scores = dot_nt(read, write[0:16])
    time = iota(square, 0)
    pre_grads = []
    for s in range(taps - 1):
        inside = (time >= s) & (doc_col == doc_col[s : s + 1])
        spread = jnp.where(inside, log_decay - log_decay[s : s + 1], 0.0)
        weighted = jnp.where(inside, jnp.exp(spread), 0.0) * scores[:, s : s + 1]
        weighted = weighted.astype(BF16).astype(F32)
        value_grad = jnp.sum(weighted * grad_wide, axis=0, keepdims=True)
        g = gate[s : s + 1]
        slope = g * (1.0 + preact[s : s + 1] * (1.0 - g))
        pre_grad = value_grad * step[s : s + 1] * slope
        pre_grads.append(jnp.where(opening[s : s + 1], pre_grad, 0.0))
    lines = jnp.zeros((docs, nstate), F32)
    for j in range(taps - 1):
        line = jnp.zeros((1, channels), F32)
        for k in range(taps - 1 - j, taps):
            line = line + tap_ref[k : k + 1] * pre_grads[j - (taps - 1) + k]
        line = jnp.where(owner, jnp.broadcast_to(line, (docs, channels)), 0.0).astype(BF16)
        lines = lines + dot_nt(line, one_hot(lane == j * rows_in + lane_of))
    for d in range(docs):
        conv_ref[d] = jnp.broadcast_to(lines[d : d + 1], (8, nstate)).astype(BF16)


def project_body(got_ref, tokens_ref, state_ref, conv_ref, out_ref):
    parts = out_ref.shape[0]
    rows = got_ref.shape[1]
    summed = jnp.sum(got_ref[...].astype(F32), axis=0)
    high = summed.astype(BF16).astype(F32)
    both = jnp.concatenate([high, summed - high], axis=0).astype(BF16)
    partial = dot(both, tokens_ref[...])
    partial = (partial[:rows] + partial[rows:]).astype(BF16)
    width = partial.shape[1] // parts
    for d in range(parts):
        out_ref[d, 0:8] = state_ref[d]
        out_ref[d, 8:16] = partial[:, d * width : (d + 1) * width]
        out_ref[d, 16:24] = conv_ref[d]


def place_body(carry_ref, got_ref, state_ref, conv_ref, copies_ref):
    rows = got_ref.shape[0]
    state_ref[...] = jnp.zeros_like(state_ref)
    conv_ref[...] = jnp.zeros_like(conv_ref)
    total = jnp.zeros((8, got_ref.shape[2]), F32)
    for r in range(rows):
        slot = carry_ref[r]
        total = total + got_ref[r, 8:16].astype(F32)

        @pl.when(slot >= 0)
        def _():
            state_ref[slot] = got_ref[r, 0:8]
            conv_ref[slot] = got_ref[r, 16:24]

    for i in range(copies_ref.shape[0]):
        copies_ref[i] = total


def final_body(index_ref, got_ref, out_ref):
    rows_own = out_ref.shape[0]
    parts, rows, lanes = got_ref.shape
    flat = got_ref[...].reshape(parts * rows, lanes)
    want = index_ref[0] * rows_own + iota((8, lanes), 0)
    select = jnp.where(iota((8, lanes), 1) == want, 1.0, 0.0)
    out_ref[...] = dot_nt(select, flat, lax.Precision.HIGHEST)[:rows_own]


def exchange(value, axis):
    return lax.all_to_all(value, axis, split_axis=0, concat_axis=0, tiled=True)


def shards(
    tokens_in,
    mix_in,
    step_size,
    doc_ids,
    out_grad,
    proj_weight,
    conv_weight,
    decay_rate,
    carried_state,
    carried_conv,
    carry_from,
):
    _, length, model_width = tokens_in.shape
    slots, heads, part_p, nstate = carried_state.shape
    taps = conv_weight.shape[0]
    parts = lax.axis_size("fsdp")
    tokens = tokens_in[0]
    rows_in = heads * part_p

    flat_conv = carried_conv.reshape(slots, 1, (taps - 1) * rows_in)
    flat_conv = jnp.pad(flat_conv, ((0, 0), (0, 7), (0, nstate - flat_conv.shape[2])))
    stored = jnp.concatenate([carried_state.reshape(slots, rows_in, nstate), flat_conv], axis=1)
    picked = call(pick_body, shaped(stored.shape, BF16), "sv")(carry_from, stored)
    start = exchange(picked, "doc")

    turned = call(turn_body, shaped((parts, 8, proj_weight.shape[0]), BF16), "v")(proj_weight)
    weight = exchange(turned, "fsdp")
    column = call(coeff_body, shaped((parts, 8, length), BF16), "vv")(weight, tokens)
    coeff = exchange(column, "fsdp")

    coeff_part, state_part, conv_part = call(
        row_body,
        (
            shaped((parts, 8, length), BF16),
            shaped((slots, 8, nstate), BF16),
            shaped((slots, 8, nstate), BF16),
        ),
        "svvvvvvv",
        (pltpu.VMEM((length + 8, mix_in.shape[2]), F32), pltpu.VMEM((length + 8, mix_in.shape[2]), F32)),
    )(decay_rate, coeff, mix_in[0], step_size[0], doc_ids, out_grad[0], conv_weight, start)
    coeff_got = exchange(coeff_part, "fsdp")
    back = call(project_body, shaped((slots, 24, nstate), BF16), "vvvv")(
        coeff_got, tokens, state_part, conv_part
    )
    back_got = exchange(back, "doc")
    grad_state, grad_conv, copies = call(
        place_body,
        (
            shaped((slots, 8, nstate), BF16),
            shaped((slots, 8, nstate), BF16),
            shaped((parts, 8, nstate), F32),
        ),
        "sv",
    )(carry_from, back_got)
    got = exchange(copies, "fsdp")
    index = lax.axis_index("fsdp").astype(jnp.int32).reshape(1)
    grad_proj = call(final_body, shaped((model_width // (parts * slots), 2 * nstate), F32), "sv")(
        index, got
    )
    grad_state = grad_state.reshape(carried_state.shape)
    grad_conv = grad_conv[:, 0, : (taps - 1) * rows_in].reshape(carried_conv.shape)
    return (grad_proj, grad_state, grad_conv)


def solution(mesh):
    return jax.shard_map(
        shards,
        mesh=mesh,
        in_specs=(
            P("doc", None, None),
            P("doc", None, "fsdp"),
            P("doc", None, "fsdp"),
            P("doc", None),
            P("doc", None, "fsdp"),
            P("fsdp", None),
            P(None, "fsdp"),
            P("fsdp"),
            P(None, "fsdp", "doc", None),
            P(None, None, "fsdp", "doc"),
            P(),
        ),
        out_specs=(
            P(("doc", "fsdp"), None),
            P(None, "fsdp", "doc", None),
            P(None, None, "fsdp", "doc"),
        ),
        check_vma=False,
    )
```

time: 599 us -> 172 us (0.29)
  the two profiles are of different devices: /device:TPU:6 before, /device:TPU:1 now
where the time goes in v1:
time: 172 us; the launch traced here: 171 us
  blocking collectives  81.3 us (47%)
  waiting for transfers between devices  40.6 us (24%)
  starting transfers between devices  27.7 us (16%)
  Pallas kernels  16.4 us (10%)
  local copies, waits for them, and re-layouts  3.72 us (2%)
    all_to_all x3, blocking collectives, exchange(): return lax.all_to_all(value, axis, split_axis=0, concat_axis=0, tiled=True)  81.3 us
    all_to_all x3, waiting for transfers between devices, exchange(): return lax.all_to_all(value, axis, split_axis=0, concat_axis=0, tiled=True)  40.6 us
    all_to_all x3, starting transfers between devices, exchange(): return lax.all_to_all(value, axis, split_axis=0, concat_axis=0, tiled=True)  27.7 us
    pallas_call x1, Pallas kernels, shards(): call(row_body, (shaped((parts, 8, length), BF16), shaped((slots, 8, nstat...  3.93 us
  transfers between devices with their start and end apart: 3, of which 3 were waited for; matrix products, arithmetic and copies ran while one was open for 2% of the time, Pallas kernels for 1%

profile of v1, /device:TPU:1, one launch (start us, length us, event | category | flops | bytes accessed | tf_op | source)
XLA Modules:
  0.0 171.2 jit_solution(17190570138733343454)
XLA Ops:
  0.6 0.0 copy-start.4
  0.6 0.0 copy-start.3
  0.7 0.0 copy-start.5
  0.7 1.6 shard_map.130
  2.3 25.8 %all_to_all.30.weight_ref = bf16[32,8,128]{2,1,0:T(8,128)(2,1)} all-to-all(bf16[32,8,128]{2,1,0:T(8,128)(2,1)} %shard_map.130), channel_id=1, replica_groups=mesh['doc'=32,'fsdp'=32] {'fsdp'}, dimensions={0} | all-to-all | bytes 131072 | tf_op jit(solution)/shard_map/all_to_all | solution.py:258
  28.0 2.9 %shard_map.131 = bf16[32,8,256]{2,1,0:T(8,128)(2,1)} custom-call(bf16[32,8,128]{2,1,0:T(8,128)(2,1)} %all_to_all.30.weight_ref, bf16[256,4096]{1,0:T(8,128)(2,1)} %bitcast.9), custom_call_target="tpu_custom_call" | custom-call | tf_op jit(solution)/shard_map/pallas_call | solution.py:289
  31.0 3.9 %all-to-all-start.1 = ((bf16[32,8,256]{2,1,0:T(8,128)(2,1)}), bf16[32,8,256]{2,1,0:T(8,128)(2,1)S(1)}, u32[]{:S(2)}, u32[]{:S(2)}) async-start(bf16[32,8,256]{2,1,0:T(8,128)(2,1)} %shard_map.131), calls=%async_computation.1 | async-start | bytes 262144 | tf_op jit(solution)/shard_map/all_to_all | solution.py:258
  34.9 0.0 copy-done.4
  34.9 0.1 copy.18
  35.0 0.0 copy-done.3
  35.0 0.7 fusion.1.slots_ref
  35.7 1.6 shard_map.132
  37.3 5.4 %all-to-all-done.1.coeff_ref = bf16[32,8,256]{2,1,0:T(8,128)(2,1)S(1)} async-done(((bf16[32,8,256]{2,1,0:T(8,128)(2,1)}), bf16[32,8,256]{2,1,0:T(8,128)(2,1)S(1)}, u32[]{:S(2)}, u32[]{:S(2)}) %all-to-all-start.1) | async-done | bytes 131104 | tf_op jit(solution)/shard_map/all_to_all | solution.py:258
  42.7 0.0 copy-start.1
  42.7 18.7 %all-to-all-start.2 = ((bf16[32,16,128]{2,1,0:T(8,128)(2,1)}), bf16[32,16,128]{2,1,0:T(8,128)(2,1)S(1)}, u32[]{:S(2)}, u32[]{:S(2)}) async-start(bf16[32,16,128]{2,1,0:T(8,128)(2,1)} %shard_map.132), calls=%async_computation.2 | async-start | bytes 262144 | tf_op jit(solution)/shard_map/all_to_all | solution.py:258
  61.4 0.0 copy-done.5
  61.4 0.8 copy.17
  62.2 29.0 %all-to-all-done.2.start_ref = bf16[32,16,128]{2,1,0:T(8,128)(2,1)S(1)} async-done(((bf16[32,16,128]{2,1,0:T(8,128)(2,1)}), bf16[32,16,128]{2,1,0:T(8,128)(2,1)S(1)}, u32[]{:S(2)}, u32[]{:S(2)}) %all-to-all-start.2) | async-done | bytes 131104 | tf_op jit(solution)/shard_map/all_to_all | solution.py:258
  91.2 0.0 copy-start.2
  91.2 0.0 copy-done.1
  91.2 0.6 copy-done.2
  91.9 3.9 %shard_map.133 = (bf16[32,8,256]{2,1,0:T(8,128)(2,1)}, bf16[32,8,128]{2,1,0:T(8,128)(2,1)}, bf16[32,8,128]{2,1,0:T(8,128)(2,1)}) custom-call(f32[4]{0:T(128)} %decay_ref.1, bf16[32,8,256]{2,1,0:T(8,128)(2,1)} %copy-done.1, bf16[256,256]{1,0:T(8,128)(2,1)} %bitcast.12, f32[256,4]{1,0:T(8,128)} %bitcast.11, s32[1,256]{1,0:T(1,128)} %doc_ref.1, ...), custom_call_target="tpu_custom_call" | custom-call | tf_op jit(solution)/shard_map/pallas_call | solution.py:292
  95.8 14.5 %all_to_all.31.got_ref = bf16[32,8,256]{2,1,0:T(8,128)(2,1)} all-to-all(bf16[32,8,256]{2,1,0:T(8,128)(2,1)} %get-tuple-element.9), channel_id=1, replica_groups=mesh['doc'=32,'fsdp'=32] {'fsdp'}, dimensions={0} | all-to-all | bytes 262144 | tf_op jit(solution)/shard_map/all_to_all | solution.py:258
  110.4 2.7 %shard_map.134 = bf16[32,24,128]{2,1,0:T(8,128)(2,1)} custom-call(bf16[32,8,256]{2,1,0:T(8,128)(2,1)} %all_to_all.31.got_ref, bf16[256,4096]{1,0:T(8,128)(2,1)} %bitcast.10, bf16[32,8,128]{2,1,0:T(8,128)(2,1)} %get-tuple-element.10.state_ref, bf16[32,8,128]{2,1,0:T(8,128)(2,1)} %get-tuple-element.11.conv_ref), custom_call_target="tpu_custom_call" | custom-call | tf_op jit(solution)/shard_map/pallas_call | solution.py:303
  113.0 41.0 %all_to_all.32.got_ref = bf16[32,24,128]{2,1,0:T(8,128)(2,1)} all-to-all(bf16[32,24,128]{2,1,0:T(8,128)(2,1)} %shard_map.134), channel_id=1, replica_groups=mesh['doc'=32,'fsdp'=32] {'doc'}, dimensions={0} | all-to-all | bytes 393216 | tf_op jit(solution)/shard_map/all_to_all | solution.py:258
  154.1 1.9 %shard_map.135 = (bf16[32,8,128]{2,1,0:T(8,128)(2,1)}, bf16[32,8,128]{2,1,0:T(8,128)(2,1)}, f32[32,8,128]{2,1,0:T(8,128)}) custom-call(s32[32]{0:T(128)} %carry_ref.3, bf16[32,24,128]{2,1,0:T(8,128)(2,1)} %all_to_all.32.got_ref), custom_call_target="tpu_custom_call" | custom-call | tf_op jit(solution)/shard_map/pallas_call | solution.py:307
  156.0 5.1 %all-to-all-start.5 = ((f32[32,8,128]{2,1,0:T(8,128)}), f32[32,8,128]{2,1,0:T(8,128)S(1)}, u32[]{:S(2)}, u32[]{:S(2)}) async-start(f32[32,8,128]{2,1,0:T(8,128)} %get-tuple-element.12), calls=%async_computation.5 | async-start | bytes 262144 | tf_op jit(solution)/shard_map/all_to_all | solution.py:258
  161.0 0.9 slice.3
  161.9 0.7 copy.19
  162.6 6.3 %all-to-all-done.5.got_ref = f32[32,8,128]{2,1,0:T(8,128)S(1)} async-done(((f32[32,8,128]{2,1,0:T(8,128)}), f32[32,8,128]{2,1,0:T(8,128)S(1)}, u32[]{:S(2)}, u32[]{:S(2)}) %all-to-all-start.5) | async-done | bytes 131104 | tf_op jit(solution)/shard_map/all_to_all | solution.py:258
  168.8 0.0 copy-start
  168.8 0.6 copy-done
  169.5 1.7 %shard_map.136 = f32[4,256]{1,0:T(4,128)} custom-call(s32[1]{0:T(128)} %bitcast.index_ref, f32[32,8,128]{2,1,0:T(8,128)} %copy-done), custom_call_target="tpu_custom_call" | custom-call | tf_op jit(solution)/shard_map/pallas_call | solution.py:318
Async XLA Ops:
  0.6 34.2 %copy-start.4 = (bf16[32,3,4,2]{0,3,2,1:T(2,128)(2,1)S(1)}, bf16[32,3,4,2]{0,3,2,1:T(2,128)(2,1)}, u32[]{:S(2)}) copy-start(bf16[32,3,4,2]{0,3,2,1:T(2,128)(2,1)} %param.20) | copy-start | bytes 4612
  0.6 34.3 %copy-start.3 = (bf16[32,4,2,128]{3,2,1,0:T(2,128)(2,1)S(1)}, bf16[32,4,2,128]{3,2,1,0:T(2,128)(2,1)}, u32[]{:S(2)}) copy-start(bf16[32,4,2,128]{3,2,1,0:T(2,128)(2,1)} %param.19) | copy-start | bytes 196612
  0.7 60.8 %copy-start.5 = (f32[1,256,4]{1,2,0:T(4,128)S(1)}, f32[1,256,4]{1,2,0:T(4,128)}, u32[]{:S(2)}) copy-start(f32[1,256,4]{1,2,0:T(4,128)} %param.13) | copy-start | bytes 12292
  31.0 11.7 %all-to-all-start.1 = ((bf16[32,8,256]{2,1,0:T(8,128)(2,1)}), bf16[32,8,256]{2,1,0:T(8,128)(2,1)S(1)}, u32[]{:S(2)}, u32[]{:S(2)}) async-start(bf16[32,8,256]{2,1,0:T(8,128)(2,1)} %shard_map.131), calls=%async_computation.1 | async-start | bytes 262144 | tf_op jit(solution)/shard_map/all_to_all | solution.py:258
  42.7 48.6 %copy-start.1 = (bf16[32,8,256]{2,1,0:T(8,128)(2,1)}, bf16[32,8,256]{2,1,0:T(8,128)(2,1)S(1)}, u32[]{:S(2)}) copy-start(bf16[32,8,256]{2,1,0:T(8,128)(2,1)S(1)} %all-to-all-done.1.coeff_ref) | copy-start | bytes 393220
  42.7 48.6 %all-to-all-start.2 = ((bf16[32,16,128]{2,1,0:T(8,128)(2,1)}), bf16[32,16,128]{2,1,0:T(8,128)(2,1)S(1)}, u32[]{:S(2)}, u32[]{:S(2)}) async-start(bf16[32,16,128]{2,1,0:T(8,128)(2,1)} %shard_map.132), calls=%async_computation.2 | async-start | bytes 262144 | tf_op jit(solution)/shard_map/all_to_all | solution.py:258
  91.2 0.6 copy-start.2
  156.0 12.9 %all-to-all-start.5 = ((f32[32,8,128]{2,1,0:T(8,128)}), f32[32,8,128]{2,1,0:T(8,128)S(1)}, u32[]{:S(2)}, u32[]{:S(2)}) async-start(f32[32,8,128]{2,1,0:T(8,128)} %get-tuple-element.12), calls=%async_computation.5 | async-start | bytes 262144 | tf_op jit(solution)/shard_map/all_to_all | solution.py:258
  168.8 0.7 copy-start

commit v2 on v1

--- a/solution.py
+++ b/solution.py
@@ -1,9 +1,12 @@
+import functools
+
 import jax
 import jax.numpy as jnp
 from jax import lax
 from jax.experimental import pallas as pl
 from jax.experimental.pallas import tpu as pltpu
 from jax.sharding import PartitionSpec as P
+
 
 INTERPRET = False
 F32 = jnp.float32
@@ -72,18 +75,19 @@
         copies_ref[i] = column
 
 
-def row_body(
+def early_body(
     decay_ref,
-    coeff_ref,
     mix_ref,
     step_ref,
     doc_ref,
     grad_ref,
     tap_ref,
     start_ref,
-    coeff_grad_ref,
-    state_ref,
-    conv_ref,
+    score_ref,
+    scaled_ref,
+    carried_ref,
+    reach_ref,
+    slope_ref,
     ext,
     doc_ext,
 ):
@@ -91,26 +95,21 @@
     heads = step_ref.shape[1]
     head_dim = channels // heads
     taps = tap_ref.shape[0]
-    docs = start_ref.shape[0]
+    all_rows, nstate = start_ref.shape
+    per_doc = slope_ref.shape[1]
+    docs = all_rows // per_doc
     part_p = head_dim // docs
     rows_in = heads * part_p
-    nstate = start_ref.shape[2]
     square = (length, channels)
 
-    start = start_ref[...].astype(F32)
-    state_in = start[:, :rows_in].reshape(channels, nstate).astype(BF16)
-    conv_in = jnp.sum(start[:, rows_in:], axis=1).astype(BF16)
-    chan = iota((channels, channels), 0)
-    other = iota((channels, channels), 1)
+    start = start_ref[...]
+    chan = iota((channels, all_rows), 0)
     place = (
-        ((chan % head_dim) // part_p) * rows_in + (chan // head_dim) * part_p + chan % part_p
-    )
-    to_natural = one_hot(place == other)
-    place_t = (
-        ((other % head_dim) // part_p) * rows_in + (other // head_dim) * part_p + other % part_p
-    )
-    to_parts = one_hot(place_t == chan)
-    state_zero = dot(to_natural, state_in).astype(BF16)
+        ((chan % head_dim) // part_p) * per_doc + (chan // head_dim) * part_p + chan % part_p
+    )
+    state_zero = dot(one_hot(place == iota((channels, all_rows), 1)), start).astype(BF16)
+    conv_row = iota((docs, all_rows), 0) * per_doc + rows_in
+    conv_in = dot(one_hot(conv_row == iota((docs, all_rows), 1)), start).astype(BF16)
     lane_chan = iota((nstate, channels), 1)
     lane = iota((nstate, channels), 0)
     lane_of = (lane_chan // head_dim) * part_p + lane_chan % part_p
@@ -146,20 +145,20 @@
     gate = 1.0 / (1.0 + jnp.exp(-preact))
     mixed = (preact * gate).astype(BF16).astype(F32)
     values = (step * mixed).astype(BF16)
+    g = gate[0:8]
+    slope = step[0:8] * g * (1.0 + preact[0:8] * (1.0 - g))
+    slope_ref[0, 0:8] = jnp.where(opening[0:8], slope, 0.0)
 
     time_row = iota((length, length), 0)
-    time_col = iota((length, length), 1)
-    lower = time_row >= time_col
+    lower = time_row >= iota((length, length), 1)
     lower_one = one_hot(lower)
     change = -(rate * step)
     first = change.astype(BF16)
-    rest = change - first.astype(F32)
-    second, third = halves(rest)
+    second, third = halves(change - first.astype(F32))
     log_decay = dot(lower_one, first) + (dot(lower_one, second) + dot(lower_one, third))
     log_turned = log_decay.T
     allowed = lower & (doc_col == doc_row.astype(F32))
-    grad = grad_ref[...]
-    grad_wide = grad.astype(F32)
+    grad_wide = grad_ref[...].astype(F32)
     score_grad = jnp.zeros((length, length), F32)
     for h in range(heads):
         own = jnp.where(head_of == h, grad_wide, 0.0).astype(BF16)
@@ -168,39 +167,74 @@
         spread = column - log_turned[h * head_dim : h * head_dim + 1]
         decays = jnp.where(allowed, jnp.exp(jnp.where(allowed, spread, 0.0)), 0.0)
         score_grad = score_grad + decays * products
-
+    score_high, score_low = halves(score_grad)
+    score_ref[0] = score_high
+    score_ref[1] = score_low
+    edge = jnp.where(opening, jnp.exp(log_decay), 0.0)
+    scaled_high, scaled_low = halves(edge * grad_wide)
+    scaled_ref[0] = scaled_high
+    scaled_ref[1] = scaled_low
+    carried_ref[...] = dot(scaled_high, state_zero) + dot(scaled_low, state_zero)
+
+    time = iota(square, 0)
+    for s in range(taps - 1):
+        inside = (time >= s) & (doc_col == doc_col[s : s + 1])
+        spread = jnp.where(inside, log_decay - log_decay[s : s + 1], 0.0)
+        reach_ref[s] = jnp.where(inside, jnp.exp(spread) * grad_wide, 0.0).astype(BF16)
+
+
+def late_body(
+    heads,
+    coeff_ref,
+    score_ref,
+    scaled_ref,
+    carried_ref,
+    reach_ref,
+    slope_ref,
+    tap_ref,
+    coeff_grad_ref,
+    state_ref,
+    conv_ref,
+):
+    _, length, channels = scaled_ref.shape
+    nstate = carried_ref.shape[1]
+    docs, rows_in, _ = state_ref.shape
+    taps = tap_ref.shape[0]
     coeff = coeff_ref[...].astype(F32).reshape(2 * nstate, length)
+    head_dim = channels // heads
+    part_p = head_dim // docs
     write_turned = coeff[:nstate]
     read_turned = coeff[nstate:]
     write = write_turned.T.astype(BF16)
-    read = read_turned.T.astype(BF16)
     read_turned = read_turned.astype(BF16)
-
-    edge = jnp.where(opening, jnp.exp(log_decay), 0.0)
-    scaled_high, scaled_low = halves(edge * grad_wide)
-    score_high, score_low = halves(score_grad)
-    read_grad = dot(score_high, write) + dot(score_low, write)
-    read_grad = read_grad + dot(scaled_high, state_zero) + dot(scaled_low, state_zero)
+    score_high = score_ref[0]
+    score_low = score_ref[1]
+    scaled_high = scaled_ref[0]
+    scaled_low = scaled_ref[1]
+    read_grad = dot(score_high, write) + dot(score_low, write) + carried_ref[...]
     write_grad = dot(read_turned, score_high) + dot(read_turned, score_low)
     coeff_grad = jnp.concatenate([write_grad, read_grad.T], axis=0)
     coeff_grad_ref[...] = coeff_grad.reshape(coeff_grad_ref.shape).astype(BF16)
     state_grad = dot(read_turned, scaled_high) + dot(read_turned, scaled_low)
     state_grad = state_grad.T.astype(BF16)
+    chan = iota((channels, channels), 1)
+    place = (
+        ((chan % head_dim) // part_p) * rows_in + (chan // head_dim) * part_p + chan % part_p
+    )
+    to_parts = one_hot(place == iota((channels, channels), 0))
     state_ref[...] = dot(to_parts, state_grad).reshape(state_ref.shape).astype(BF16)
 
-    scores = dot_nt(read, write[0:16])
-    time = iota(square, 0)
+    scores = dot(write[0:16], read_turned)
+    score_high, score_low = halves(scores)
     pre_grads = []
     for s in range(taps - 1):
-        inside = (time >= s) & (doc_col == doc_col[s : s + 1])
-        spread = jnp.where(inside, log_decay - log_decay[s : s + 1], 0.0)
-        weighted = jnp.where(inside, jnp.exp(spread), 0.0) * scores[:, s : s + 1]
-        weighted = weighted.astype(BF16).astype(F32)
-        value_grad = jnp.sum(weighted * grad_wide, axis=0, keepdims=True)
-        g = gate[s : s + 1]
-        slope = g * (1.0 + preact[s : s + 1] * (1.0 - g))
-        pre_grad = value_grad * step[s : s + 1] * slope
-        pre_grads.append(jnp.where(opening[s : s + 1], pre_grad, 0.0))
+        reach = reach_ref[s]
+        value_grad = dot(score_high, reach) + dot(score_low, reach)
+        pre_grads.append(value_grad[s : s + 1] * slope_ref[0, s : s + 1])
+    lane_chan = iota((nstate, channels), 1)
+    lane = iota((nstate, channels), 0)
+    lane_of = (lane_chan // head_dim) * part_p + lane_chan % part_p
+    owner = (iota((docs, channels), 1) % head_dim) // part_p == iota((docs, channels), 0)
     lines = jnp.zeros((docs, nstate), F32)
     for j in range(taps - 1):
         line = jnp.zeros((1, channels), F32)
@@ -208,11 +242,10 @@
             line = line + tap_ref[k : k + 1] * pre_grads[j - (taps - 1) + k]
         line = jnp.where(owner, jnp.broadcast_to(line, (docs, channels)), 0.0).astype(BF16)
         lines = lines + dot_nt(line, one_hot(lane == j * rows_in + lane_of))
-    for d in range(docs):
-        conv_ref[d] = jnp.broadcast_to(lines[d : d + 1], (8, nstate)).astype(BF16)
-
-
-def project_body(got_ref, tokens_ref, state_ref, conv_ref, out_ref):
+    conv_ref[...] = lines.astype(BF16)
+
+
+def project_body(got_ref, tokens_ref, out_ref):
     parts = out_ref.shape[0]
     rows = got_ref.shape[1]
     summed = jnp.sum(got_ref[...].astype(F32), axis=0)
@@ -222,25 +255,25 @@
     partial = (partial[:rows] + partial[rows:]).astype(BF16)
     width = partial.shape[1] // parts
     for d in range(parts):
-        out_ref[d, 0:8] = state_ref[d]
-        out_ref[d, 8:16] = partial[:, d * width : (d + 1) * width]
-        out_ref[d, 16:24] = conv_ref[d]
-
-
-def place_body(carry_ref, got_ref, state_ref, conv_ref, copies_ref):
-    rows = got_ref.shape[0]
+        out_ref[d] = partial[:, d * width : (d + 1) * width]
+
+
+def place_body(carry_ref, got_ref, flat_ref, state_ref, conv_ref, copies_ref):
+    rows, pairs, _, _ = got_ref.shape
+    kept = state_ref.shape[1]
     state_ref[...] = jnp.zeros_like(state_ref)
     conv_ref[...] = jnp.zeros_like(conv_ref)
-    total = jnp.zeros((8, got_ref.shape[2]), F32)
     for r in range(rows):
         slot = carry_ref[r]
-        total = total + got_ref[r, 8:16].astype(F32)
 
         @pl.when(slot >= 0)
         def _():
-            state_ref[slot] = got_ref[r, 0:8]
-            conv_ref[slot] = got_ref[r, 16:24]
-
+            state_ref[slot] = got_ref[r, 0:kept]
+            conv_ref[slot] = got_ref[r, pairs - 1 : pairs]
+
+    every = flat_ref.shape[0]
+    mine = iota((8, every), 1) % (2 * pairs) == 2 * kept + iota((8, every), 0)
+    total = dot(one_hot(mine), flat_ref[...])
     for i in range(copies_ref.shape[0]):
         copies_ref[i] = total
 
@@ -278,48 +311,68 @@
     tokens = tokens_in[0]
     rows_in = heads * part_p
 
-    flat_conv = carried_conv.reshape(slots, 1, (taps - 1) * rows_in)
-    flat_conv = jnp.pad(flat_conv, ((0, 0), (0, 7), (0, nstate - flat_conv.shape[2])))
-    stored = jnp.concatenate([carried_state.reshape(slots, rows_in, nstate), flat_conv], axis=1)
+    flat_conv = carried_conv.reshape(slots, 1, 1, (taps - 1) * rows_in)
+    flat_conv = jnp.pad(flat_conv, ((0, 0), (0, 0), (0, 1), (0, nstate - flat_conv.shape[3])))
+    stored = carried_state.reshape(slots, rows_in // 2, 2, nstate)
+    stored = jnp.concatenate([stored, flat_conv], axis=1)
     picked = call(pick_body, shaped(stored.shape, BF16), "sv")(carry_from, stored)
-    start = exchange(picked, "doc")
+    start = exchange(picked, "doc").reshape(slots * (rows_in + 2), nstate)
 
     turned = call(turn_body, shaped((parts, 8, proj_weight.shape[0]), BF16), "v")(proj_weight)
     weight = exchange(turned, "fsdp")
     column = call(coeff_body, shaped((parts, 8, length), BF16), "vv")(weight, tokens)
     coeff = exchange(column, "fsdp")
 
+    channels = mix_in.shape[2]
+    kept = call(
+        early_body,
+        (
+            shaped((2, length, length), BF16),
+            shaped((2, length, channels), BF16),
+            shaped((length, nstate), F32),
+            shaped((taps - 1, length, channels), BF16),
+            shaped((1, rows_in + 2, channels), F32),
+        ),
+        "svvvvvv",
+        (pltpu.VMEM((length + 8, channels), F32), pltpu.VMEM((length + 8, channels), F32)),
+    )(decay_rate, mix_in[0], step_size[0], doc_ids, out_grad[0], conv_weight, start)
     coeff_part, state_part, conv_part = call(
-        row_body,
+        functools.partial(late_body, heads),
         (
             shaped((parts, 8, length), BF16),
-            shaped((slots, 8, nstate), BF16),
-            shaped((slots, 8, nstate), BF16),
+            shaped((slots, rows_in, nstate), BF16),
+            shaped((slots, nstate), BF16),
         ),
-        "svvvvvvv",
-        (pltpu.VMEM((length + 8, mix_in.shape[2]), F32), pltpu.VMEM((length + 8, mix_in.shape[2]), F32)),
-    )(decay_rate, coeff, mix_in[0], step_size[0], doc_ids, out_grad[0], conv_weight, start)
+        "vvvvvvv",
+    )(coeff, *kept, conv_weight)
     coeff_got = exchange(coeff_part, "fsdp")
-    back = call(project_body, shaped((slots, 24, nstate), BF16), "vvvv")(
-        coeff_got, tokens, state_part, conv_part
+    share = call(project_body, shaped((slots, 8, nstate), BF16), "vv")(coeff_got, tokens)
+    conv_part = jnp.pad(conv_part.reshape(slots, 1, 1, nstate), ((0, 0), (0, 0), (0, 1), (0, 0)))
+    back = jnp.concatenate(
+        [
+            state_part.reshape(slots, rows_in // 2, 2, nstate),
+            share.reshape(slots, 4, 2, nstate),
+            conv_part,
+        ],
+        axis=1,
     )
     back_got = exchange(back, "doc")
     grad_state, grad_conv, copies = call(
         place_body,
         (
-            shaped((slots, 8, nstate), BF16),
-            shaped((slots, 8, nstate), BF16),
+            shaped((slots, rows_in // 2, 2, nstate), BF16),
+            shaped((slots, 1, 2, nstate), BF16),
             shaped((parts, 8, nstate), F32),
         ),
-        "sv",
-    )(carry_from, back_got)
+        "svv",
+    )(carry_from, back_got, back_got.reshape(-1, nstate))
     got = exchange(copies, "fsdp")
     index = lax.axis_index("fsdp").astype(jnp.int32).reshape(1)
-    grad_proj = call(final_body, shaped((model_width // (parts * slots), 2 * nstate), F32), "sv")(
-        index, got
-    )
+    grad_proj = call(
+        final_body, shaped((model_width // (parts * slots), 2 * nstate), F32), "sv"
+    )(index, got)
     grad_state = grad_state.reshape(carried_state.shape)
-    grad_conv = grad_conv[:, 0, : (taps - 1) * rows_in].reshape(carried_conv.shape)
+    grad_conv = grad_conv[:, 0, 0, : (taps - 1) * rows_in].reshape(carried_conv.shape)
     return (grad_proj, grad_state, grad_conv)
 
 

time: 172 us -> 160 us (0.930)
  blocking collectives: 81.3 us -> 35.1 us
  starting transfers between devices: 27.7 us -> 52.9 us
  waiting for transfers between devices: 40.6 us -> 43.5 us
  Pallas kernels: 16.4 us -> 18.6 us
  local copies, waits for them, and re-layouts: 3.72 us -> 5.63 us
  other arithmetic: 0.68 us -> 2.52 us
    all_to_all x3 -> x1, blocking collectives: 81.3 us -> 35.1 us  [exchange(): return lax.all_to_all(value, axis, split_axis=0, concat_axis=0, tiled=True)]
    all_to_all x3 -> x5, starting transfers between devices: 27.7 us -> 52.9 us  [exchange(): return lax.all_to_all(value, axis, split_axis=0, concat_axis=0, tiled=True)]
    all_to_all x3 -> x5, waiting for transfers between devices: 40.6 us -> 43.5 us  [exchange(): return lax.all_to_all(value, axis, split_axis=0, concat_axis=0, tiled=True)]
    pallas_call x3 -> x4, Pallas kernels: 8.48 us -> 10.7 us  [the longest x1 3.19 us: shards(): call(early_body, (shaped((2, length, length), BF16), shaped((2, length, c...]
    concatenate x1 -> x2, other arithmetic: 0.68 us -> 2.52 us  [the longest x1 1.55 us: shards(): stored = jnp.concatenate([stored, flat_conv], axis=1)]
  transfers between devices with their start and end apart: 3 -> 5, of which waited for: 3 -> 5; matrix products, arithmetic and copies ran while one was open for 2% -> 3% of each run, Pallas kernels for 1% -> 5%
where the time goes in v2:
time: 160 us; the launch traced here: 159 us
  starting transfers between devices  52.9 us (33%)
  waiting for transfers between devices  43.5 us (27%)
  blocking collectives  35.1 us (22%)
  Pallas kernels  18.6 us (12%)
  local copies, waits for them, and re-layouts  5.63 us (4%)
  other arithmetic  2.52 us (2%)
    all_to_all x5, starting transfers between devices, exchange(): return lax.all_to_all(value, axis, split_axis=0, concat_axis=0, tiled=True)  52.9 us
    all_to_all x5, waiting for transfers between devices, exchange(): return lax.all_to_all(value, axis, split_axis=0, concat_axis=0, tiled=True)  43.5 us
    all_to_all x1, blocking collectives, exchange(): return lax.all_to_all(value, axis, split_axis=0, concat_axis=0, tiled=True)  35.1 us
  transfers between devices with their start and end apart: 5, of which 5 were waited for; matrix products, arithmetic and copies ran while one was open for 3% of the time, Pallas kernels for 5%

profile of v2, /device:TPU:1, one launch (start us, length us, event | category | flops | bytes accessed | tf_op | source)
XLA Modules:
  0.0 158.9 jit_solution(289650313503206313)
XLA Ops:
  0.6 0.0 copy-start.6
  0.6 1.6 shard_map.130
  2.2 17.6 %all-to-all-start = ((bf16[32,8,128]{2,1,0:T(8,128)(2,1)}), bf16[32,8,128]{2,1,0:T(8,128)(2,1)S(1)}, u32[]{:S(2)}, u32[]{:S(2)}) async-start(bf16[32,8,128]{2,1,0:T(8,128)(2,1)} %shard_map.130), calls=%async_computation | async-start | bytes 131072 | tf_op jit(solution)/shard_map/all_to_all | solution.py:291
  19.8 0.8 copy.18
  20.6 1.5 fusion.1.slots_ref
  22.2 1.6 %shard_map.132 = bf16[32,5,2,128]{3,2,1,0:T(2,128)(2,1)} custom-call(s32[32]{0:T(128)} %carry_ref.3, bf16[32,5,2,128]{3,2,1,0:T(2,128)(2,1)} %fusion.1.slots_ref), custom_call_target="tpu_custom_call" | custom-call | tf_op jit(solution)/shard_map/pallas_call | solution.py:318
  23.8 3.5 %all-to-all-done.weight_ref = bf16[32,8,128]{2,1,0:T(8,128)(2,1)S(1)} async-done(((bf16[32,8,128]{2,1,0:T(8,128)(2,1)}), bf16[32,8,128]{2,1,0:T(8,128)(2,1)S(1)}, u32[]{:S(2)}, u32[]{:S(2)}) %all-to-all-start) | async-done | bytes 65568 | tf_op jit(solution)/shard_map/all_to_all | solution.py:291
  27.3 0.0 copy-start.4
  27.3 19.3 %all-to-all-start.2 = ((bf16[32,5,2,128]{3,2,1,0:T(2,128)(2,1)}), bf16[32,5,2,128]{3,2,1,0:T(2,128)(2,1)S(1)}, u32[]{:S(2)}, u32[]{:S(2)}) async-start(bf16[32,5,2,128]{3,2,1,0:T(2,128)(2,1)} %shard_map.132), calls=%async_computation.2 | async-start | bytes 163840 | tf_op jit(solution)/shard_map/all_to_all | solution.py:291
  46.6 0.0 copy-done.4
  46.6 2.9 %shard_map.131 = bf16[32,8,256]{2,1,0:T(8,128)(2,1)} custom-call(bf16[32,8,128]{2,1,0:T(8,128)(2,1)} %copy-done.4, bf16[256,4096]{1,0:T(8,128)(2,1)} %bitcast.13), custom_call_target="tpu_custom_call" | custom-call | tf_op jit(solution)/shard_map/pallas_call | solution.py:323
  49.6 22.8 %all-to-all-done.2 = bf16[32,5,2,128]{3,2,1,0:T(2,128)(2,1)S(1)} async-done(((bf16[32,5,2,128]{3,2,1,0:T(2,128)(2,1)}), bf16[32,5,2,128]{3,2,1,0:T(2,128)(2,1)S(1)}, u32[]{:S(2)}, u32[]{:S(2)}) %all-to-all-start.2) | async-done | bytes 81952 | tf_op jit(solution)/shard_map/all_to_all | solution.py:291
  72.4 0.0 copy-start.3
  72.4 6.1 %all-to-all-start.1 = ((bf16[32,8,256]{2,1,0:T(8,128)(2,1)}), bf16[32,8,256]{2,1,0:T(8,128)(2,1)S(1)}, u32[]{:S(2)}, u32[]{:S(2)}) async-start(bf16[32,8,256]{2,1,0:T(8,128)(2,1)} %shard_map.131), calls=%async_computation.1 | async-start | bytes 262144 | tf_op jit(solution)/shard_map/all_to_all | solution.py:291
  78.5 0.0 copy-done.6
  78.5 0.8 copy.17
  79.3 0.0 copy-done.3
  79.3 3.2 %shard_map.133 = (bf16[2,256,256]{2,1,0:T(8,128)(2,1)}, bf16[2,256,256]{2,1,0:T(8,128)(2,1)}, f32[256,128]{1,0:T(8,128)}, bf16[3,256,256]{2,1,0:T(8,128)(2,1)}, f32[1,10,256]{2,1,0:T(8,128)}) custom-call(f32[4]{0:T(128)} %decay_ref.1, bf16[256,256]{1,0:T(8,128)(2,1)} %bitcast.19, f32[256,4]{1,0:T(8,128)} %bitcast.16, s32[1,256]{1,0:T(1,128)} %doc_ref.1, ...), custom_call_target="tpu_custom_call" | custom-call | tf_op jit(solution)/shard_map/pallas_call | solution.py:327
  82.5 3.7 %all-to-all-done.1.coeff_ref = bf16[32,8,256]{2,1,0:T(8,128)(2,1)S(1)} async-done(((bf16[32,8,256]{2,1,0:T(8,128)(2,1)}), bf16[32,8,256]{2,1,0:T(8,128)(2,1)S(1)}, u32[]{:S(2)}, u32[]{:S(2)}) %all-to-all-start.1) | async-done | bytes 131104 | tf_op jit(solution)/shard_map/all_to_all | solution.py:291
  86.2 0.0 copy-start
  86.2 0.6 copy-done
  86.8 2.8 %shard_map.134 = (bf16[32,8,256]{2,1,0:T(8,128)(2,1)}, bf16[32,8,128]{2,1,0:T(8,128)(2,1)}, bf16[32,128]{1,0:T(8,128)(2,1)}) custom-call(bf16[32,8,256]{2,1,0:T(8,128)(2,1)} %copy-done, bf16[2,256,256]{2,1,0:T(8,128)(2,1)} %get-tuple-element.14.score_ref, bf16[2,256,256]{2,1,0:T(8,128)(2,1)} %get-tuple-element.15.scaled_ref, ...), custom_call_target="tpu_custom_call" | custom-call | tf_op jit(solution)/shard_map/pallas_call | solution.py:339
  89.6 0.0 copy-start.5
  89.6 4.0 %all-to-all-start.3 = ((bf16[32,8,256]{2,1,0:T(8,128)(2,1)}), bf16[32,8,256]{2,1,0:T(8,128)(2,1)S(1)}, u32[]{:S(2)}, u32[]{:S(2)}) async-start(bf16[32,8,256]{2,1,0:T(8,128)(2,1)} %get-tuple-element.20), calls=%async_computation.3 | async-start | bytes 262144 | tf_op jit(solution)/shard_map/all_to_all | solution.py:291
  93.6 0.7 copy.19
  94.3 7.1 %all-to-all-done.3.got_ref = bf16[32,8,256]{2,1,0:T(8,128)(2,1)S(1)} async-done(((bf16[32,8,256]{2,1,0:T(8,128)(2,1)}), bf16[32,8,256]{2,1,0:T(8,128)(2,1)S(1)}, u32[]{:S(2)}, u32[]{:S(2)}) %all-to-all-start.3) | async-done | bytes 131104 | tf_op jit(solution)/shard_map/all_to_all | solution.py:291
  101.4 0.0 copy-start.1
  101.4 0.7 copy-done.1
  102.1 2.7 %shard_map.135 = bf16[32,8,128]{2,1,0:T(8,128)(2,1)} custom-call(bf16[32,8,256]{2,1,0:T(8,128)(2,1)} %copy-done.1, bf16[256,4096]{1,0:T(8,128)(2,1)} %bitcast.14), custom_call_target="tpu_custom_call" | custom-call | tf_op jit(solution)/shard_map/pallas_call | solution.py:349
  104.8 0.0 copy-done.5
  104.8 1.0 fusion
  105.8 35.1 %all_to_all.30.got_ref = bf16[32,9,2,128]{3,2,1,0:T(2,128)(2,1)} all-to-all(bf16[32,9,2,128]{3,2,1,0:T(2,128)(2,1)S(1)} %fusion), channel_id=1, replica_groups=mesh['doc'=32,'fsdp'=32] {'doc'}, dimensions={0} | all-to-all | bytes 294912 | tf_op jit(solution)/shard_map/all_to_all | solution.py:291
  140.8 2.1 %shard_map.136 = (bf16[32,4,2,128]{3,2,1,0:T(2,128)(2,1)}, bf16[32,1,2,128]{3,2,1,0:T(2,128)(2,1)}, f32[32,8,128]{2,1,0:T(8,128)}) custom-call(s32[32]{0:T(128)} %carry_ref.3, bf16[32,9,2,128]{3,2,1,0:T(2,128)(2,1)} %all_to_all.30.got_ref, bf16[576,128]{1,0:T(8,128)(2,1)} %bitcast.15), custom_call_target="tpu_custom_call" | custom-call | tf_op jit(solution)/shard_map/pallas_call | solution.py:360
  142.9 5.8 %all-to-all-start.5 = ((f32[32,8,128]{2,1,0:T(8,128)}), f32[32,8,128]{2,1,0:T(8,128)S(1)}, u32[]{:S(2)}, u32[]{:S(2)}) async-start(f32[32,8,128]{2,1,0:T(8,128)} %get-tuple-element.22), calls=%async_computation.5 | async-start | bytes 262144 | tf_op jit(solution)/shard_map/all_to_all | solution.py:291
  148.7 1.4 copy.20
  150.1 6.4 %all-to-all-done.5.got_ref = f32[32,8,128]{2,1,0:T(8,128)S(1)} async-done(((f32[32,8,128]{2,1,0:T(8,128)}), f32[32,8,128]{2,1,0:T(8,128)S(1)}, u32[]{:S(2)}, u32[]{:S(2)}) %all-to-all-start.5) | async-done | bytes 131104 | tf_op jit(solution)/shard_map/all_to_all | solution.py:291
  156.5 0.0 copy-start.2
  156.5 0.7 copy-done.2
  157.2 1.7 %shard_map.137 = f32[4,256]{1,0:T(4,128)} custom-call(s32[1]{0:T(128)} %bitcast.index_ref, f32[32,8,128]{2,1,0:T(8,128)} %copy-done.2), custom_call_target="tpu_custom_call" | custom-call | tf_op jit(solution)/shard_map/pallas_call | solution.py:371
Async XLA Ops:
  0.6 77.8 %copy-start.6 = (f32[1,256,4]{1,2,0:T(4,128)S(1)}, f32[1,256,4]{1,2,0:T(4,128)}, u32[]{:S(2)}) copy-start(f32[1,256,4]{1,2,0:T(4,128)} %param.13) | copy-start | bytes 12292
  2.2 25.1 %all-to-all-start = ((bf16[32,8,128]{2,1,0:T(8,128)(2,1)}), bf16[32,8,128]{2,1,0:T(8,128)(2,1)S(1)}, u32[]{:S(2)}, u32[]{:S(2)}) async-start(bf16[32,8,128]{2,1,0:T(8,128)(2,1)} %shard_map.130), calls=%async_computation | async-start | bytes 131072 | tf_op jit(solution)/shard_map/all_to_all | solution.py:291
  27.3 19.3 %copy-start.4 = (bf16[32,8,128]{2,1,0:T(8,128)(2,1)}, bf16[32,8,128]{2,1,0:T(8,128)(2,1)S(1)}, u32[]{:S(2)}) copy-start(bf16[32,8,128]{2,1,0:T(8,128)(2,1)S(1)} %all-to-all-done.weight_ref) | copy-start | bytes 196612
  27.3 45.1 %all-to-all-start.2 = ((bf16[32,5,2,128]{3,2,1,0:T(2,128)(2,1)}), bf16[32,5,2,128]{3,2,1,0:T(2,128)(2,1)S(1)}, u32[]{:S(2)}, u32[]{:S(2)}) async-start(bf16[32,5,2,128]{3,2,1,0:T(2,128)(2,1)} %shard_map.132), calls=%async_computation.2 | async-start | bytes 163840 | tf_op jit(solution)/shard_map/all_to_all | solution.py:291
  72.4 6.9 %copy-start.3 = (bf16[32,5,2,128]{3,2,1,0:T(2,128)(2,1)}, bf16[32,5,2,128]{3,2,1,0:T(2,128)(2,1)S(1)}, u32[]{:S(2)}) copy-start(bf16[32,5,2,128]{3,2,1,0:T(2,128)(2,1)S(1)} %all-to-all-done.2) | copy-start | bytes 245764
  72.4 13.8 %all-to-all-start.1 = ((bf16[32,8,256]{2,1,0:T(8,128)(2,1)}), bf16[32,8,256]{2,1,0:T(8,128)(2,1)S(1)}, u32[]{:S(2)}, u32[]{:S(2)}) async-start(bf16[32,8,256]{2,1,0:T(8,128)(2,1)} %shard_map.131), calls=%async_computation.1 | async-start | bytes 262144 | tf_op jit(solution)/shard_map/all_to_all | solution.py:291
  86.2 0.6 copy-start
  89.6 15.2 %copy-start.5 = (bf16[32,8,128]{2,1,0:T(8,128)(2,1)S(1)}, bf16[32,8,128]{2,1,0:T(8,128)(2,1)}, u32[]{:S(2)}) copy-start(bf16[32,8,128]{2,1,0:T(8,128)(2,1)} %get-tuple-element.19) | copy-start | bytes 196612
  89.6 11.8 %all-to-all-start.3 = ((bf16[32,8,256]{2,1,0:T(8,128)(2,1)}), bf16[32,8,256]{2,1,0:T(8,128)(2,1)S(1)}, u32[]{:S(2)}, u32[]{:S(2)}) async-start(bf16[32,8,256]{2,1,0:T(8,128)(2,1)} %get-tuple-element.20), calls=%async_computation.3 | async-start | bytes 262144 | tf_op jit(solution)/shard_map/all_to_all | solution.py:291
  101.4 0.7 copy-start.1
  142.9 13.6 %all-to-all-start.5 = ((f32[32,8,128]{2,1,0:T(8,128)}), f32[32,8,128]{2,1,0:T(8,128)S(1)}, u32[]{:S(2)}, u32[]{:S(2)}) async-start(f32[32,8,128]{2,1,0:T(8,128)} %get-tuple-element.22), calls=%async_computation.5 | async-start | bytes 262144 | tf_op jit(solution)/shard_map/all_to_all | solution.py:291
  156.5 0.7 copy-start.2

commit v3 on v2

--- a/solution.py
+++ b/solution.py
@@ -9,6 +9,7 @@
 
 
 INTERPRET = False
+LIMIT = 24 * 1024 * 1024
 F32 = jnp.float32
 BF16 = jnp.bfloat16
 
@@ -46,6 +47,7 @@
         in_specs=[smem if spec == "s" else vmem for spec in in_specs],
         out_specs=tuple(vmem for _ in out_shape) if many else vmem,
         scratch_shapes=list(scratch),
+        compiler_params=pltpu.CompilerParams(vmem_limit_bytes=LIMIT),
         interpret=INTERPRET,
     )
 
@@ -183,39 +185,29 @@
         reach_ref[s] = jnp.where(inside, jnp.exp(spread) * grad_wide, 0.0).astype(BF16)
 
 
-def late_body(
-    heads,
-    coeff_ref,
-    score_ref,
-    scaled_ref,
-    carried_ref,
-    reach_ref,
-    slope_ref,
-    tap_ref,
-    coeff_grad_ref,
-    state_ref,
-    conv_ref,
-):
+def columns_body(coeff_ref, score_ref, carried_ref, coeff_grad_ref):
+    length, nstate = carried_ref.shape
+    coeff = coeff_ref[...].astype(F32).reshape(2 * nstate, length)
+    write = coeff[:nstate].T.astype(BF16)
+    read_turned = coeff[nstate:].astype(BF16)
+    score_high = score_ref[0]
+    score_low = score_ref[1]
+    read_grad = dot(score_high, write) + dot(score_low, write) + carried_ref[...]
+    write_grad = dot(read_turned, score_high) + dot(read_turned, score_low)
+    coeff_grad = jnp.concatenate([write_grad, read_grad.T], axis=0)
+    coeff_grad_ref[...] = coeff_grad.reshape(coeff_grad_ref.shape).astype(BF16)
+
+
+def state_body(heads, coeff_ref, scaled_ref, reach_ref, slope_ref, tap_ref, state_ref, conv_ref):
     _, length, channels = scaled_ref.shape
-    nstate = carried_ref.shape[1]
-    docs, rows_in, _ = state_ref.shape
+    docs, rows_in, nstate = state_ref.shape
     taps = tap_ref.shape[0]
     coeff = coeff_ref[...].astype(F32).reshape(2 * nstate, length)
     head_dim = channels // heads
     part_p = head_dim // docs
-    write_turned = coeff[:nstate]
-    read_turned = coeff[nstate:]
-    write = write_turned.T.astype(BF16)
-    read_turned = read_turned.astype(BF16)
-    score_high = score_ref[0]
-    score_low = score_ref[1]
-    scaled_high = scaled_ref[0]
-    scaled_low = scaled_ref[1]
-    read_grad = dot(score_high, write) + dot(score_low, write) + carried_ref[...]
-    write_grad = dot(read_turned, score_high) + dot(read_turned, score_low)
-    coeff_grad = jnp.concatenate([write_grad, read_grad.T], axis=0)
-    coeff_grad_ref[...] = coeff_grad.reshape(coeff_grad_ref.shape).astype(BF16)
-    state_grad = dot(read_turned, scaled_high) + dot(read_turned, scaled_low)
+    write = coeff[:nstate].T.astype(BF16)
+    read_turned = coeff[nstate:].astype(BF16)
+    state_grad = dot(read_turned, scaled_ref[0]) + dot(read_turned, scaled_ref[1])
     state_grad = state_grad.T.astype(BF16)
     chan = iota((channels, channels), 1)
     place = (
@@ -245,20 +237,33 @@
     conv_ref[...] = lines.astype(BF16)
 
 
-def project_body(got_ref, tokens_ref, out_ref):
+def project_body(got_ref, tokens_ref, state_ref, conv_ref, out_ref):
     parts = out_ref.shape[0]
+    kept = state_ref.shape[1]
     rows = got_ref.shape[1]
     summed = jnp.sum(got_ref[...].astype(F32), axis=0)
     high = summed.astype(BF16).astype(F32)
     both = jnp.concatenate([high, summed - high], axis=0).astype(BF16)
     partial = dot(both, tokens_ref[...])
-    partial = (partial[:rows] + partial[rows:]).astype(BF16)
+    partial = partial[:rows] + partial[rows:]
     width = partial.shape[1] // parts
+    out_ref[:, 0:kept] = state_ref[...]
+    out_ref[:, kept + rows // 2 :] = conv_ref[...]
     for d in range(parts):
-        out_ref[d] = partial[:, d * width : (d + 1) * width]
-
-
-def place_body(carry_ref, got_ref, flat_ref, state_ref, conv_ref, copies_ref):
+        block = partial[:, d * width : (d + 1) * width]
+        for k in range(rows // 2):
+            out_ref[d, kept + k] = block[2 * k : 2 * k + 2].astype(BF16)
+
+
+def total_body(pairs, kept, flat_ref, copies_ref):
+    every = flat_ref.shape[0]
+    mine = iota((8, every), 1) % (2 * pairs) == 2 * kept + iota((8, every), 0)
+    total = dot(one_hot(mine), flat_ref[...])
+    for i in range(copies_ref.shape[0]):
+        copies_ref[i] = total
+
+
+def place_body(carry_ref, got_ref, state_ref, conv_ref):
     rows, pairs, _, _ = got_ref.shape
     kept = state_ref.shape[1]
     state_ref[...] = jnp.zeros_like(state_ref)
@@ -270,12 +275,6 @@
         def _():
             state_ref[slot] = got_ref[r, 0:kept]
             conv_ref[slot] = got_ref[r, pairs - 1 : pairs]
-
-    every = flat_ref.shape[0]
-    mine = iota((8, every), 1) % (2 * pairs) == 2 * kept + iota((8, every), 0)
-    total = dot(one_hot(mine), flat_ref[...])
-    for i in range(copies_ref.shape[0]):
-        copies_ref[i] = total
 
 
 def final_body(index_ref, got_ref, out_ref):
@@ -336,37 +335,30 @@
         "svvvvvv",
         (pltpu.VMEM((length + 8, channels), F32), pltpu.VMEM((length + 8, channels), F32)),
     )(decay_rate, mix_in[0], step_size[0], doc_ids, out_grad[0], conv_weight, start)
-    coeff_part, state_part, conv_part = call(
-        functools.partial(late_body, heads),
-        (
-            shaped((parts, 8, length), BF16),
-            shaped((slots, rows_in, nstate), BF16),
-            shaped((slots, nstate), BF16),
-        ),
-        "vvvvvvv",
-    )(coeff, *kept, conv_weight)
+    scores, scaled, carried, reach, slope = kept
+    coeff_part = call(columns_body, shaped((parts, 8, length), BF16), "vvv")(coeff, scores, carried)
     coeff_got = exchange(coeff_part, "fsdp")
-    share = call(project_body, shaped((slots, 8, nstate), BF16), "vv")(coeff_got, tokens)
+    state_part, conv_part = call(
+        functools.partial(state_body, heads),
+        (shaped((slots, rows_in, nstate), BF16), shaped((slots, nstate), BF16)),
+        "vvvvv",
+    )(coeff, scaled, reach, slope, conv_weight)
+    state_pairs = rows_in // 2
     conv_part = jnp.pad(conv_part.reshape(slots, 1, 1, nstate), ((0, 0), (0, 0), (0, 1), (0, 0)))
-    back = jnp.concatenate(
-        [
-            state_part.reshape(slots, rows_in // 2, 2, nstate),
-            share.reshape(slots, 4, 2, nstate),
-            conv_part,
-        ],
-        axis=1,
+    pairs = state_pairs + 5
+    back = call(project_body, shaped((slots, pairs, 2, nstate), BF16), "vvvv")(
+        coeff_got, tokens, state_part.reshape(slots, state_pairs, 2, nstate), conv_part
     )
     back_got = exchange(back, "doc")
-    grad_state, grad_conv, copies = call(
+    copies = call(
+        functools.partial(total_body, pairs, state_pairs), shaped((parts, 8, nstate), F32), "v"
+    )(back_got.reshape(-1, nstate))
+    got = exchange(copies, "fsdp")
+    grad_state, grad_conv = call(
         place_body,
-        (
-            shaped((slots, rows_in // 2, 2, nstate), BF16),
-            shaped((slots, 1, 2, nstate), BF16),
-            shaped((parts, 8, nstate), F32),
-        ),
-        "svv",
-    )(carry_from, back_got, back_got.reshape(-1, nstate))
-    got = exchange(copies, "fsdp")
+        (shaped((slots, state_pairs, 2, nstate), BF16), shaped((slots, 1, 2, nstate), BF16)),
+        "sv",
+    )(carry_from, back_got)
     index = lax.axis_index("fsdp").astype(jnp.int32).reshape(1)
     grad_proj = call(
         final_body, shaped((model_width // (parts * slots), 2 * nstate), F32), "sv"

time: 160 us -> 151 us (0.944)
  Pallas kernels: 18.6 us -> 10.4 us
    pallas_call x3 -> x5, Pallas kernels: 7.55 us -> 4.37 us  [the longest x1 1.42 us: shards(): call(place_body, (shaped((slots, state_pairs, 2, nstate), BF16), shaped((...]
    unnamed x15 -> x27, local copies, waits for them, and re-layouts: 2.75 us -> 5.71 us
    pallas_call x1, Pallas kernels: 2.93 us -> 1.31 us  [shards(): call(coeff_body, shaped((parts, 8, length), BF16), 'vv')(weight, tokens)]
  transfers between devices with their start and end apart: 5 -> 5, of which waited for: 5 -> 5; matrix products, arithmetic and copies ran while one was open for 3% -> 2% of each run, Pallas kernels for 5% -> 4%
where the time goes in v3:
time: 151 us; the launch traced here: 150 us
  starting transfers between devices  52.6 us (35%)
  waiting for transfers between devices  43.5 us (29%)
  blocking collectives  34.4 us (23%)
  Pallas kernels  10.4 us (7%)
  local copies, waits for them, and re-layouts  7.22 us (5%)
    all_to_all x5, starting transfers between devices, exchange(): return lax.all_to_all(value, axis, split_axis=0, concat_axis=0, tiled=True)  52.6 us
    all_to_all x5, waiting for transfers between devices, exchange(): return lax.all_to_all(value, axis, split_axis=0, concat_axis=0, tiled=True)  43.5 us
    all_to_all x1, blocking collectives, exchange(): return lax.all_to_all(value, axis, split_axis=0, concat_axis=0, tiled=True)  34.4 us
    unnamed x27, local copies, waits for them, and re-layouts  5.71 us
  transfers between devices with their start and end apart: 5, of which 5 were waited for; matrix products, arithmetic and copies ran while one was open for 2% of the time, Pallas kernels for 4%

profile of v3, /device:TPU:1, one launch (start us, length us, event | category | flops | bytes accessed | tf_op | source)
XLA Modules:
  0.0 149.9 jit_solution(7505512719446680937)
XLA Ops:
  0.6 0.0 copy-start.2
  0.6 0.0 copy-start.6
  0.7 0.9 copy-done.6
  1.5 0.0 copy-start.12
  1.5 0.0 copy-start.7
  1.5 0.0 copy-start.10
  1.5 0.0 copy-start.11
  1.5 0.7 shard_map.130
  2.3 17.6 %all-to-all-start = ((bf16[32,8,128]{2,1,0:T(8,128)(2,1)}), bf16[32,8,128]{2,1,0:T(8,128)(2,1)S(1)}, u32[]{:S(2)}, u32[]{:S(2)}) async-start(bf16[32,8,128]{2,1,0:T(8,128)(2,1)} %shard_map.130), calls=%async_computation | async-start | bytes 131072 | tf_op jit(solution)/shard_map/all_to_all | solution.py:290
  19.9 0.8 copy.18
  20.7 0.9 fusion.slots_ref
  21.6 0.0 copy-start.8
  21.6 0.6 copy-done.8
  22.3 1.3 shard_map.132
  23.6 3.8 %all-to-all-done.weight_ref = bf16[32,8,128]{2,1,0:T(8,128)(2,1)S(1)} async-done(((bf16[32,8,128]{2,1,0:T(8,128)(2,1)}), bf16[32,8,128]{2,1,0:T(8,128)(2,1)S(1)}, u32[]{:S(2)}, u32[]{:S(2)}) %all-to-all-start) | async-done | bytes 65568 | tf_op jit(solution)/shard_map/all_to_all | solution.py:290
  27.4 19.3 %all-to-all-start.2 = ((bf16[32,5,2,128]{3,2,1,0:T(2,128)(2,1)}), bf16[32,5,2,128]{3,2,1,0:T(2,128)(2,1)S(1)}, u32[]{:S(2)}, u32[]{:S(2)}) async-start(bf16[32,5,2,128]{3,2,1,0:T(2,128)(2,1)} %shard_map.132), calls=%async_computation.2 | async-start | bytes 163840 | tf_op jit(solution)/shard_map/all_to_all | solution.py:290
  46.7 0.0 copy-start
  46.7 1.6 %copy-done = bf16[1,256,4096]{2,1,0:T(8,128)(2,1)S(1)} copy-done((bf16[1,256,4096]{2,1,0:T(8,128)(2,1)S(1)}, bf16[1,256,4096]{2,1,0:T(8,128)(2,1)}, u32[]{:S(2)}) %copy-start) | copy-done | bytes 2097176
  48.3 0.0 copy-start.1
  48.3 1.3 shard_map.131
  49.6 22.9 %all-to-all-done.2 = bf16[32,5,2,128]{3,2,1,0:T(2,128)(2,1)S(1)} async-done(((bf16[32,5,2,128]{3,2,1,0:T(2,128)(2,1)}), bf16[32,5,2,128]{3,2,1,0:T(2,128)(2,1)S(1)}, u32[]{:S(2)}, u32[]{:S(2)}) %all-to-all-start.2) | async-done | bytes 81952 | tf_op jit(solution)/shard_map/all_to_all | solution.py:290
  72.4 6.0 %all-to-all-start.1 = ((bf16[32,8,256]{2,1,0:T(8,128)(2,1)}), bf16[32,8,256]{2,1,0:T(8,128)(2,1)S(1)}, u32[]{:S(2)}, u32[]{:S(2)}) async-start(bf16[32,8,256]{2,1,0:T(8,128)(2,1)} %shard_map.131), calls=%async_computation.1 | async-start | bytes 262144 | tf_op jit(solution)/shard_map/all_to_all | solution.py:290
  78.4 0.0 copy-done.12
  78.4 0.1 copy.17
  78.6 0.0 copy-done.2
  78.6 0.0 copy-done.7
  78.6 0.0 copy-done.10
  78.6 0.0 copy-done.11
  78.6 0.0 copy-start.3
  78.6 0.9 copy-done.3
  79.5 1.9 %shard_map.133 = (bf16[2,256,256]{2,1,0:T(8,128)(2,1)S(1)}, bf16[2,256,256]{2,1,0:T(8,128)(2,1)S(1)}, f32[256,128]{1,0:T(8,128)S(1)}, bf16[3,256,256]{2,1,0:T(8,128)(2,1)S(1)}, f32[1,10,256]{2,1,0:T(8,128)S(1)}) custom-call(f32[4]{0:T(128)S(1)} %copy-done.11, bf16[256,256]{1,0:T(8,128)(2,1)S(1)} %bitcast.17, f32[256,4]{1,0:T(8,128)S(1)} %bitcast.15, ...), custom_call_target="tpu_custom_call" | custom-call | tf_op jit(solution)/shard_map/pallas_call | solution.py:326
  81.4 0.0 copy-start.4
  81.4 0.6 copy-done.4
  82.1 4.1 %all-to-all-done.1.coeff_ref = bf16[32,8,256]{2,1,0:T(8,128)(2,1)S(1)} async-done(((bf16[32,8,256]{2,1,0:T(8,128)(2,1)}), bf16[32,8,256]{2,1,0:T(8,128)(2,1)S(1)}, u32[]{:S(2)}, u32[]{:S(2)}) %all-to-all-start.1) | async-done | bytes 131104 | tf_op jit(solution)/shard_map/all_to_all | solution.py:290
  86.2 0.0 copy-start.5
  86.2 0.9 copy-done.5
  87.1 1.1 shard_map.134
  88.2 3.9 %all-to-all-start.3 = ((bf16[32,8,256]{2,1,0:T(8,128)(2,1)}), bf16[32,8,256]{2,1,0:T(8,128)(2,1)S(1)}, u32[]{:S(2)}, u32[]{:S(2)}) async-start(bf16[32,8,256]{2,1,0:T(8,128)(2,1)} %shard_map.134), calls=%async_computation.3 | async-start | bytes 262144 | tf_op jit(solution)/shard_map/all_to_all | solution.py:290
  92.1 0.0 copy-start.9
  92.1 0.7 shard_map.135
  92.9 7.0 %all-to-all-done.3.got_ref = bf16[32,8,256]{2,1,0:T(8,128)(2,1)S(1)} async-done(((bf16[32,8,256]{2,1,0:T(8,128)(2,1)}), bf16[32,8,256]{2,1,0:T(8,128)(2,1)S(1)}, u32[]{:S(2)}, u32[]{:S(2)}) %all-to-all-start.3) | async-done | bytes 131104 | tf_op jit(solution)/shard_map/all_to_all | solution.py:290
  99.9 0.0 copy-done.1
  99.9 0.4 shard_map.136
  100.3 34.4 %all_to_all.30.got_ref = bf16[32,9,2,128]{3,2,1,0:T(2,128)(2,1)S(1)} all-to-all(bf16[32,9,2,128]{3,2,1,0:T(2,128)(2,1)S(1)} %shard_map.136), channel_id=1, replica_groups=mesh['doc'=32,'fsdp'=32] {'doc'}, dimensions={0} | all-to-all | bytes 294912 | tf_op jit(solution)/shard_map/all_to_all | solution.py:290
  134.7 0.8 shard_map.137
  135.5 5.9 %all-to-all-start.5 = ((f32[32,8,128]{2,1,0:T(8,128)}), f32[32,8,128]{2,1,0:T(8,128)S(1)}, u32[]{:S(2)}, u32[]{:S(2)}) async-start(f32[32,8,128]{2,1,0:T(8,128)} %shard_map.137), calls=%async_computation.5 | async-start | bytes 262144 | tf_op jit(solution)/shard_map/all_to_all | solution.py:290
  141.3 0.0 copy-done.9
  141.3 1.4 shard_map.139
  142.8 0.7 copy.20
  143.4 5.7 %all-to-all-done.5.got_ref = f32[32,8,128]{2,1,0:T(8,128)S(1)} async-done(((f32[32,8,128]{2,1,0:T(8,128)}), f32[32,8,128]{2,1,0:T(8,128)S(1)}, u32[]{:S(2)}, u32[]{:S(2)}) %all-to-all-start.5) | async-done | bytes 131104 | tf_op jit(solution)/shard_map/all_to_all | solution.py:290
  149.1 0.8 shard_map.138
  (2 shorter events, 0.1 us)
Async XLA Ops:
  0.6 77.9 %copy-start.2 = (bf16[1,256,256]{2,1,0:T(8,128)(2,1)S(1)}, bf16[1,256,256]{2,1,0:T(8,128)(2,1)}, u32[]{:S(2)}) copy-start(bf16[1,256,256]{2,1,0:T(8,128)(2,1)} %param.12) | copy-start | bytes 393220
  0.6 0.9 copy-start.6
  1.5 76.9 %copy-start.12 = (f32[1,256,4]{1,2,0:T(4,128)S(1)}, f32[1,256,4]{1,2,0:T(4,128)}, u32[]{:S(2)}) copy-start(f32[1,256,4]{1,2,0:T(4,128)} %param.13) | copy-start | bytes 12292
  1.5 77.1 %copy-start.7 = (f32[4,256]{1,0:T(4,128)S(1)}, f32[4,256]{1,0:T(4,128)}, u32[]{:S(2)}) copy-start(f32[4,256]{1,0:T(4,128)} %tap_ref.3) | copy-start | bytes 12292
  1.5 77.1 %copy-start.10 = (s32[1,256]{1,0:T(1,128)S(1)}, s32[1,256]{1,0:T(1,128)}, u32[]{:S(2)}) copy-start(s32[1,256]{1,0:T(1,128)} %doc_ref.1) | copy-start | bytes 3076
  1.5 77.1 %copy-start.11 = (f32[4]{0:T(128)S(1)}, f32[4]{0:T(128)}, u32[]{:S(2)}) copy-start(f32[4]{0:T(128)} %decay_ref.1) | copy-start | bytes 52
  2.3 25.1 %all-to-all-start = ((bf16[32,8,128]{2,1,0:T(8,128)(2,1)}), bf16[32,8,128]{2,1,0:T(8,128)(2,1)S(1)}, u32[]{:S(2)}, u32[]{:S(2)}) async-start(bf16[32,8,128]{2,1,0:T(8,128)(2,1)} %shard_map.130), calls=%async_computation | async-start | bytes 131072 | tf_op jit(solution)/shard_map/all_to_all | solution.py:290
  21.6 0.7 copy-start.8
  27.4 45.1 %all-to-all-start.2 = ((bf16[32,5,2,128]{3,2,1,0:T(2,128)(2,1)}), bf16[32,5,2,128]{3,2,1,0:T(2,128)(2,1)S(1)}, u32[]{:S(2)}, u32[]{:S(2)}) async-start(bf16[32,5,2,128]{3,2,1,0:T(2,128)(2,1)} %shard_map.132), calls=%async_computation.2 | async-start | bytes 163840 | tf_op jit(solution)/shard_map/all_to_all | solution.py:290
  46.7 1.6 %copy-start = (bf16[1,256,4096]{2,1,0:T(8,128)(2,1)S(1)}, bf16[1,256,4096]{2,1,0:T(8,128)(2,1)}, u32[]{:S(2)}) copy-start(bf16[1,256,4096]{2,1,0:T(8,128)(2,1)} %param.11) | copy-start | bytes 6291460
  48.3 51.6 %copy-start.1 = (bf16[1,256,4096]{2,1,0:T(8,128)(2,1)S(1)}, bf16[1,256,4096]{2,1,0:T(8,128)(2,1)}, u32[]{:S(2)}) copy-start(bf16[1,256,4096]{2,1,0:T(8,128)(2,1)} %param.11) | copy-start | bytes 6291460
  72.4 13.8 %all-to-all-start.1 = ((bf16[32,8,256]{2,1,0:T(8,128)(2,1)}), bf16[32,8,256]{2,1,0:T(8,128)(2,1)S(1)}, u32[]{:S(2)}, u32[]{:S(2)}) async-start(bf16[32,8,256]{2,1,0:T(8,128)(2,1)} %shard_map.131), calls=%async_computation.1 | async-start | bytes 262144 | tf_op jit(solution)/shard_map/all_to_all | solution.py:290
  78.6 0.9 copy-start.3
  81.4 0.7 copy-start.4
  86.2 0.9 copy-start.5
  88.2 11.7 %all-to-all-start.3 = ((bf16[32,8,256]{2,1,0:T(8,128)(2,1)}), bf16[32,8,256]{2,1,0:T(8,128)(2,1)S(1)}, u32[]{:S(2)}, u32[]{:S(2)}) async-start(bf16[32,8,256]{2,1,0:T(8,128)(2,1)} %shard_map.134), calls=%async_computation.3 | async-start | bytes 262144 | tf_op jit(solution)/shard_map/all_to_all | solution.py:290
  92.1 49.3 %copy-start.9 = (s32[32]{0:T(128)S(1)}, s32[32]{0:T(128)}, u32[]{:S(2)}) copy-start(s32[32]{0:T(128)} %carry_ref.3) | copy-start | bytes 388
  135.5 13.7 %all-to-all-start.5 = ((f32[32,8,128]{2,1,0:T(8,128)}), f32[32,8,128]{2,1,0:T(8,128)S(1)}, u32[]{:S(2)}, u32[]{:S(2)}) async-start(f32[32,8,128]{2,1,0:T(8,128)} %shard_map.137), calls=%async_computation.5 | async-start | bytes 262144 | tf_op jit(solution)/shard_map/all_to_all | solution.py:290

commit v4 on v3

--- a/solution.py
+++ b/solution.py
@@ -174,9 +174,11 @@
     score_ref[1] = score_low
     edge = jnp.where(opening, jnp.exp(log_decay), 0.0)
     scaled_high, scaled_low = halves(edge * grad_wide)
-    scaled_ref[0] = scaled_high
-    scaled_ref[1] = scaled_low
-    carried_ref[...] = dot(scaled_high, state_zero) + dot(scaled_low, state_zero)
+    scaled_ref[...] = scaled_high
+    carried = dot(scaled_high, state_zero) + dot(scaled_low, state_zero)
+    carried_high, carried_low = halves(carried.T)
+    carried_ref[0] = carried_high
+    carried_ref[1] = carried_low
 
     time = iota(square, 0)
     for s in range(taps - 1):
@@ -186,20 +188,21 @@
 
 
 def columns_body(coeff_ref, score_ref, carried_ref, coeff_grad_ref):
-    length, nstate = carried_ref.shape
+    _, nstate, length = carried_ref.shape
     coeff = coeff_ref[...].astype(F32).reshape(2 * nstate, length)
-    write = coeff[:nstate].T.astype(BF16)
+    write_turned = coeff[:nstate].astype(BF16)
     read_turned = coeff[nstate:].astype(BF16)
     score_high = score_ref[0]
     score_low = score_ref[1]
-    read_grad = dot(score_high, write) + dot(score_low, write) + carried_ref[...]
+    read_grad = dot_nt(write_turned, score_high) + dot_nt(write_turned, score_low)
+    read_grad = read_grad + (carried_ref[0].astype(F32) + carried_ref[1].astype(F32))
     write_grad = dot(read_turned, score_high) + dot(read_turned, score_low)
-    coeff_grad = jnp.concatenate([write_grad, read_grad.T], axis=0)
+    coeff_grad = jnp.concatenate([write_grad, read_grad], axis=0)
     coeff_grad_ref[...] = coeff_grad.reshape(coeff_grad_ref.shape).astype(BF16)
 
 
 def state_body(heads, coeff_ref, scaled_ref, reach_ref, slope_ref, tap_ref, state_ref, conv_ref):
-    _, length, channels = scaled_ref.shape
+    length, channels = scaled_ref.shape
     docs, rows_in, nstate = state_ref.shape
     taps = tap_ref.shape[0]
     coeff = coeff_ref[...].astype(F32).reshape(2 * nstate, length)
@@ -207,7 +210,7 @@
     part_p = head_dim // docs
     write = coeff[:nstate].T.astype(BF16)
     read_turned = coeff[nstate:].astype(BF16)
-    state_grad = dot(read_turned, scaled_ref[0]) + dot(read_turned, scaled_ref[1])
+    state_grad = dot(read_turned, scaled_ref[...])
     state_grad = state_grad.T.astype(BF16)
     chan = iota((channels, channels), 1)
     place = (
@@ -327,8 +330,8 @@
         early_body,
         (
             shaped((2, length, length), BF16),
-            shaped((2, length, channels), BF16),
-            shaped((length, nstate), F32),
+            shaped((length, channels), BF16),
+            shaped((2, nstate, length), BF16),
             shaped((taps - 1, length, channels), BF16),
             shaped((1, rows_in + 2, channels), F32),
         ),

time: 151 us -> 150 us (level)
  transfers between devices with their start and end apart: 5 -> 5, of which waited for: 5 -> 5; matrix products, arithmetic and copies ran while one was open for 2% -> 2% of each run, Pallas kernels for 4% -> 5%
where the time goes in v4:
time: 150 us; the launch traced here: 149 us
  starting transfers between devices  52.8 us (35%)
  waiting for transfers between devices  43.4 us (29%)
  blocking collectives  34.4 us (23%)
  Pallas kernels  10.4 us (7%)
  local copies, waits for them, and re-layouts  6.31 us (4%)
    all_to_all x5, starting transfers between devices, exchange(): return lax.all_to_all(value, axis, split_axis=0, concat_axis=0, tiled=True)  52.8 us
    all_to_all x5, waiting for transfers between devices, exchange(): return lax.all_to_all(value, axis, split_axis=0, concat_axis=0, tiled=True)  43.4 us
    all_to_all x1, blocking collectives, exchange(): return lax.all_to_all(value, axis, split_axis=0, concat_axis=0, tiled=True)  34.4 us
    unnamed x27, local copies, waits for them, and re-layouts  4.82 us
  transfers between devices with their start and end apart: 5, of which 5 were waited for; matrix products, arithmetic and copies ran while one was open for 2% of the time, Pallas kernels for 5%

profile of v4, /device:TPU:1, one launch (start us, length us, event | category | flops | bytes accessed | tf_op | source)
XLA Modules:
  0.0 149.0 jit_solution(7489985301332810777)
XLA Ops:
  0.6 0.0 copy-start.2
  0.6 0.0 copy-start.3
  0.7 0.0 copy-start.6
  0.7 0.9 copy-done.6
  1.5 0.0 copy-start.12
  1.5 0.0 copy-start.7
  1.5 0.0 copy-start.10
  1.5 0.0 copy-start.11
  1.5 0.7 shard_map.130
  2.3 17.6 %all-to-all-start = ((bf16[32,8,128]{2,1,0:T(8,128)(2,1)}), bf16[32,8,128]{2,1,0:T(8,128)(2,1)S(1)}, u32[]{:S(2)}, u32[]{:S(2)}) async-start(bf16[32,8,128]{2,1,0:T(8,128)(2,1)} %shard_map.130), calls=%async_computation | async-start | bytes 131072 | tf_op jit(solution)/shard_map/all_to_all | solution.py:293
  19.9 0.8 copy.18
  20.7 0.9 fusion.slots_ref
  21.6 0.0 copy-start.8
  21.6 0.6 copy-done.8
  22.3 1.3 shard_map.132
  23.6 3.8 %all-to-all-done.weight_ref = bf16[32,8,128]{2,1,0:T(8,128)(2,1)S(1)} async-done(((bf16[32,8,128]{2,1,0:T(8,128)(2,1)}), bf16[32,8,128]{2,1,0:T(8,128)(2,1)S(1)}, u32[]{:S(2)}, u32[]{:S(2)}) %all-to-all-start) | async-done | bytes 65568 | tf_op jit(solution)/shard_map/all_to_all | solution.py:293
  27.4 19.3 %all-to-all-start.2 = ((bf16[32,5,2,128]{3,2,1,0:T(2,128)(2,1)}), bf16[32,5,2,128]{3,2,1,0:T(2,128)(2,1)S(1)}, u32[]{:S(2)}, u32[]{:S(2)}) async-start(bf16[32,5,2,128]{3,2,1,0:T(2,128)(2,1)} %shard_map.132), calls=%async_computation.2 | async-start | bytes 163840 | tf_op jit(solution)/shard_map/all_to_all | solution.py:293
  46.7 0.0 copy-start
  46.7 1.6 %copy-done = bf16[1,256,4096]{2,1,0:T(8,128)(2,1)S(1)} copy-done((bf16[1,256,4096]{2,1,0:T(8,128)(2,1)S(1)}, bf16[1,256,4096]{2,1,0:T(8,128)(2,1)}, u32[]{:S(2)}) %copy-start) | copy-done | bytes 2097176
  48.3 0.0 copy-start.1
  48.3 1.3 shard_map.131
  49.6 22.9 %all-to-all-done.2 = bf16[32,5,2,128]{3,2,1,0:T(2,128)(2,1)S(1)} async-done(((bf16[32,5,2,128]{3,2,1,0:T(2,128)(2,1)}), bf16[32,5,2,128]{3,2,1,0:T(2,128)(2,1)S(1)}, u32[]{:S(2)}, u32[]{:S(2)}) %all-to-all-start.2) | async-done | bytes 81952 | tf_op jit(solution)/shard_map/all_to_all | solution.py:293
  72.5 6.0 %all-to-all-start.1 = ((bf16[32,8,256]{2,1,0:T(8,128)(2,1)}), bf16[32,8,256]{2,1,0:T(8,128)(2,1)S(1)}, u32[]{:S(2)}, u32[]{:S(2)}) async-start(bf16[32,8,256]{2,1,0:T(8,128)(2,1)} %shard_map.131), calls=%async_computation.1 | async-start | bytes 262144 | tf_op jit(solution)/shard_map/all_to_all | solution.py:293
  78.4 0.0 copy-done.12
  78.4 0.1 copy.17
  78.6 0.0 copy-done.2
  78.6 0.0 copy-done.3
  78.6 0.0 copy-done.7
  78.6 0.0 copy-done.10
  78.6 0.0 copy-done.11
  78.6 1.9 %shard_map.133 = (bf16[2,256,256]{2,1,0:T(8,128)(2,1)S(1)}, bf16[256,256]{1,0:T(8,128)(2,1)S(1)}, bf16[2,128,256]{2,1,0:T(8,128)(2,1)S(1)}, bf16[3,256,256]{2,1,0:T(8,128)(2,1)S(1)}, f32[1,10,256]{2,1,0:T(8,128)S(1)}) custom-call(f32[4]{0:T(128)S(1)} %copy-done.11, bf16[256,256]{1,0:T(8,128)(2,1)S(1)} %bitcast.17, f32[256,4]{1,0:T(8,128)S(1)} %bitcast.15, ...), custom_call_target="tpu_custom_call" | custom-call | tf_op jit(solution)/shard_map/pallas_call | solution.py:329
  80.6 0.0 copy-start.4
  80.6 0.6 copy-done.4
  81.2 5.0 %all-to-all-done.1.coeff_ref = bf16[32,8,256]{2,1,0:T(8,128)(2,1)S(1)} async-done(((bf16[32,8,256]{2,1,0:T(8,128)(2,1)}), bf16[32,8,256]{2,1,0:T(8,128)(2,1)S(1)}, u32[]{:S(2)}, u32[]{:S(2)}) %all-to-all-start.1) | async-done | bytes 131104 | tf_op jit(solution)/shard_map/all_to_all | solution.py:293
  86.2 0.9 shard_map.134
  87.2 0.0 copy-start.9
  87.2 4.0 %all-to-all-start.3 = ((bf16[32,8,256]{2,1,0:T(8,128)(2,1)}), bf16[32,8,256]{2,1,0:T(8,128)(2,1)S(1)}, u32[]{:S(2)}, u32[]{:S(2)}) async-start(bf16[32,8,256]{2,1,0:T(8,128)(2,1)} %shard_map.134), calls=%async_computation.3 | async-start | bytes 262144 | tf_op jit(solution)/shard_map/all_to_all | solution.py:293
  91.2 0.0 copy-start.5
  91.2 0.9 copy-done.5
  92.1 0.8 shard_map.135
  92.9 6.0 %all-to-all-done.3.got_ref = bf16[32,8,256]{2,1,0:T(8,128)(2,1)S(1)} async-done(((bf16[32,8,256]{2,1,0:T(8,128)(2,1)}), bf16[32,8,256]{2,1,0:T(8,128)(2,1)S(1)}, u32[]{:S(2)}, u32[]{:S(2)}) %all-to-all-start.3) | async-done | bytes 131104 | tf_op jit(solution)/shard_map/all_to_all | solution.py:293
  99.0 0.0 copy-done.1
  99.0 0.4 shard_map.136
  99.4 34.4 %all_to_all.30.got_ref = bf16[32,9,2,128]{3,2,1,0:T(2,128)(2,1)S(1)} all-to-all(bf16[32,9,2,128]{3,2,1,0:T(2,128)(2,1)S(1)} %shard_map.136), channel_id=1, replica_groups=mesh['doc'=32,'fsdp'=32] {'doc'}, dimensions={0} | all-to-all | bytes 294912 | tf_op jit(solution)/shard_map/all_to_all | solution.py:293
  133.8 0.8 shard_map.137
  134.6 5.9 %all-to-all-start.5 = ((f32[32,8,128]{2,1,0:T(8,128)}), f32[32,8,128]{2,1,0:T(8,128)S(1)}, u32[]{:S(2)}, u32[]{:S(2)}) async-start(f32[32,8,128]{2,1,0:T(8,128)} %shard_map.137), calls=%async_computation.5 | async-start | bytes 262144 | tf_op jit(solution)/shard_map/all_to_all | solution.py:293
  140.4 0.0 copy-done.9
  140.5 1.4 shard_map.139
  141.9 0.7 copy.20
  142.6 5.7 %all-to-all-done.5.got_ref = f32[32,8,128]{2,1,0:T(8,128)S(1)} async-done(((f32[32,8,128]{2,1,0:T(8,128)}), f32[32,8,128]{2,1,0:T(8,128)S(1)}, u32[]{:S(2)}, u32[]{:S(2)}) %all-to-all-start.5) | async-done | bytes 131104 | tf_op jit(solution)/shard_map/all_to_all | solution.py:293
  148.2 0.8 shard_map.138
  (2 shorter events, 0.0 us)
Async XLA Ops:
  0.6 78.0 %copy-start.2 = (bf16[1,256,256]{2,1,0:T(8,128)(2,1)S(1)}, bf16[1,256,256]{2,1,0:T(8,128)(2,1)}, u32[]{:S(2)}) copy-start(bf16[1,256,256]{2,1,0:T(8,128)(2,1)} %param.12) | copy-start | bytes 393220
  0.6 78.0 %copy-start.3 = (bf16[1,256,256]{2,1,0:T(8,128)(2,1)S(1)}, bf16[1,256,256]{2,1,0:T(8,128)(2,1)}, u32[]{:S(2)}) copy-start(bf16[1,256,256]{2,1,0:T(8,128)(2,1)} %param.15) | copy-start | bytes 393220
  0.7 0.9 copy-start.6
  1.5 76.9 %copy-start.12 = (f32[1,256,4]{1,2,0:T(4,128)S(1)}, f32[1,256,4]{1,2,0:T(4,128)}, u32[]{:S(2)}) copy-start(f32[1,256,4]{1,2,0:T(4,128)} %param.13) | copy-start | bytes 12292
  1.5 77.1 %copy-start.7 = (f32[4,256]{1,0:T(4,128)S(1)}, f32[4,256]{1,0:T(4,128)}, u32[]{:S(2)}) copy-start(f32[4,256]{1,0:T(4,128)} %tap_ref.3) | copy-start | bytes 12292
  1.5 77.1 %copy-start.10 = (s32[1,256]{1,0:T(1,128)S(1)}, s32[1,256]{1,0:T(1,128)}, u32[]{:S(2)}) copy-start(s32[1,256]{1,0:T(1,128)} %doc_ref.1) | copy-start | bytes 3076
  1.5 77.1 %copy-start.11 = (f32[4]{0:T(128)S(1)}, f32[4]{0:T(128)}, u32[]{:S(2)}) copy-start(f32[4]{0:T(128)} %decay_ref.1) | copy-start | bytes 52
  2.3 25.1 %all-to-all-start = ((bf16[32,8,128]{2,1,0:T(8,128)(2,1)}), bf16[32,8,128]{2,1,0:T(8,128)(2,1)S(1)}, u32[]{:S(2)}, u32[]{:S(2)}) async-start(bf16[32,8,128]{2,1,0:T(8,128)(2,1)} %shard_map.130), calls=%async_computation | async-start | bytes 131072 | tf_op jit(solution)/shard_map/all_to_all | solution.py:293
  21.6 0.7 copy-start.8
  27.4 45.1 %all-to-all-start.2 = ((bf16[32,5,2,128]{3,2,1,0:T(2,128)(2,1)}), bf16[32,5,2,128]{3,2,1,0:T(2,128)(2,1)S(1)}, u32[]{:S(2)}, u32[]{:S(2)}) async-start(bf16[32,5,2,128]{3,2,1,0:T(2,128)(2,1)} %shard_map.132), calls=%async_computation.2 | async-start | bytes 163840 | tf_op jit(solution)/shard_map/all_to_all | solution.py:293
  46.7 1.6 %copy-start = (bf16[1,256,4096]{2,1,0:T(8,128)(2,1)S(1)}, bf16[1,256,4096]{2,1,0:T(8,128)(2,1)}, u32[]{:S(2)}) copy-start(bf16[1,256,4096]{2,1,0:T(8,128)(2,1)} %param.11) | copy-start | bytes 6291460
  48.3 50.7 %copy-start.1 = (bf16[1,256,4096]{2,1,0:T(8,128)(2,1)S(1)}, bf16[1,256,4096]{2,1,0:T(8,128)(2,1)}, u32[]{:S(2)}) copy-start(bf16[1,256,4096]{2,1,0:T(8,128)(2,1)} %param.11) | copy-start | bytes 6291460
  72.5 13.8 %all-to-all-start.1 = ((bf16[32,8,256]{2,1,0:T(8,128)(2,1)}), bf16[32,8,256]{2,1,0:T(8,128)(2,1)S(1)}, u32[]{:S(2)}, u32[]{:S(2)}) async-start(bf16[32,8,256]{2,1,0:T(8,128)(2,1)} %shard_map.131), calls=%async_computation.1 | async-start | bytes 262144 | tf_op jit(solution)/shard_map/all_to_all | solution.py:293
  80.6 0.7 copy-start.4
  87.2 53.3 %copy-start.9 = (s32[32]{0:T(128)S(1)}, s32[32]{0:T(128)}, u32[]{:S(2)}) copy-start(s32[32]{0:T(128)} %carry_ref.3) | copy-start | bytes 388
  87.2 11.8 %all-to-all-start.3 = ((bf16[32,8,256]{2,1,0:T(8,128)(2,1)}), bf16[32,8,256]{2,1,0:T(8,128)(2,1)S(1)}, u32[]{:S(2)}, u32[]{:S(2)}) async-start(bf16[32,8,256]{2,1,0:T(8,128)(2,1)} %shard_map.134), calls=%async_computation.3 | async-start | bytes 262144 | tf_op jit(solution)/shard_map/all_to_all | solution.py:293
  91.2 0.9 copy-start.5
  134.6 13.7 %all-to-all-start.5 = ((f32[32,8,128]{2,1,0:T(8,128)}), f32[32,8,128]{2,1,0:T(8,128)S(1)}, u32[]{:S(2)}, u32[]{:S(2)}) async-start(f32[32,8,128]{2,1,0:T(8,128)} %shard_map.137), calls=%async_computation.5 | async-start | bytes 262144 | tf_op jit(solution)/shard_map/all_to_all | solution.py:293
